TPU v7x, 512 devices: a whole 4x8x8 slice. The times are simulated.
512 devices in a mesh: ctx: 128 (over x, y_lo, z, core), rec: 4 (over y_hi).
Axes of the slice: x: 4, y: 8 (y_hi: 4, y_lo: 2; y = y_hi * 2 + y_lo), z: 8, core: 2. Of those that a mesh axis runs over, the one named last changes fastest.
Arguments:
- queries: bfloat16 [4, 16384, 4096], P('rec', 'ctx'), may hold values from -6 to 6
- out_grads: bfloat16 [4, 16384, 4096], P('rec', 'ctx'), may hold values from -6 to 6
- log_sums: float32 [4, 32, 16384], P('rec', None, 'ctx'), may hold values from 1.5 to 4
- deltas: float32 [4, 32, 16384], P('rec', None, 'ctx'), may hold values from -6 to 6
- keys: bfloat16 [16384, 256], P('ctx'), may hold values from -6 to 6
- values: bfloat16 [16384, 256], P('ctx'), may hold values from -0.5 to 0.5
- doc_ids: int32 [4, 128], P('rec'), may hold values from 0 to 63, never falling along the last dimension, each value on 1 to 4 neighbouring positions
Outputs:
- query_grads: bfloat16 [4, 16384, 4096], P('rec', 'ctx')
- key_grads: bfloat16 [16384, 256], P(('ctx', 'rec'))
- value_grads: bfloat16 [16384, 256], P(('ctx', 'rec'))
Inputs may be any that keep to these rules, and one draw needn't show every extreme that they name: `doc_ids`: in each row the numbers never fall, start at 0, each document spans 1 to 4 blocks and some document spans exactly 4 blocks.
All inputs are finite; a program needn't handle non-finite values.
Results may differ from a plain program's by a relative error of at most 0.0062.
Values may be sent and summed in bfloat16 or wider, within the bound.
No kernel may reach another device: no remote copies, remote signals or barrier semaphores. Data moves between devices by JAX's collectives and lax.ppermute only.
A program may use at most 64 MiB of HBM per device.

v0:
```python
import jax
import jax.numpy as jnp
from jax import lax
from jax.sharding import PartitionSpec as P

HD = 128
MAXSPAN = 4


def shifted(block, axis, distance):
    devices = range(lax.axis_size(axis))
    route = [(i - distance, i) for i in devices if i - distance in devices]
    return lax.ppermute(block, axis, route)


def from_behind(shard, axis, by):
    peers = lax.axis_size(axis)
    return lax.ppermute(shard, axis, [(i, (i + by) % peers) for i in range(peers)])


def cut_along(shard, dim, peers):
    dims = shard.shape
    pieces = shard.reshape(*dims[:dim], peers, dims[dim] // peers, *dims[dim + 1 :])
    return jnp.moveaxis(pieces, dim, 0)


def summed_on_arrival(shard, axis, dim):
    pieces = cut_along(shard, dim, lax.axis_size(axis))
    arrived = lax.all_to_all(pieces, axis, split_axis=0, concat_axis=0, tiled=True)
    return arrived.sum(axis=0)


def sent_together(arrays, axis, dim, along):
    widths = [a.shape[along] for a in arrays]
    both = jnp.concatenate(arrays, axis=along)
    whole = summed_on_arrival(both, axis, dim)
    return tuple(jnp.split(whole, [sum(widths[:k]) for k in range(1, len(widths))], axis=along))


def tile_terms(
    query_block, grad_block, sums_block, delta_block, key_block, value_block, query_index, key_index
):
    rows = query_block.shape[0]
    key_heads = key_block.shape[1] // HD
    group = query_block.shape[1] // (key_heads * HD)
    scale = HD ** (-0.5)
    query_heads = query_block.reshape(rows, key_heads, group, HD)
    grad_heads = grad_block.reshape(rows, key_heads, group, HD)
    key_split = key_block.reshape(rows, key_heads, HD)
    value_split = value_block.reshape(rows, key_heads, HD)
    sums_heads = sums_block.reshape(key_heads, group, rows)
    delta_heads = delta_block.reshape(key_heads, group, rows)
    positions = jnp.arange(rows, dtype=jnp.int32)
    query_pos = query_index * rows + positions
    key_pos = key_index * rows + positions
    causal = key_pos[None, :] <= query_pos[:, None]
    scores = (
        jnp.einsum("qkgd,skd->kgqs", query_heads, key_split, preferred_element_type=jnp.float32)
        * scale
    )
    probs = jnp.where(causal, jnp.exp(scores - sums_heads[..., None]), 0.0)
    dprobs = jnp.einsum(
        "qkgd,skd->kgqs", grad_heads, value_split, preferred_element_type=jnp.float32
    )
    dscores = probs * (dprobs - delta_heads[..., None])
    probs_b = probs.astype(jnp.bfloat16)
    dscores_b = dscores.astype(jnp.bfloat16)
    value_grad = jnp.einsum(
        "kgqs,qkgd->skd", probs_b, grad_heads, preferred_element_type=jnp.float32
    ).reshape(rows, key_heads * HD)
    key_grad = (
        jnp.einsum(
            "kgqs,qkgd->skd", dscores_b, query_heads, preferred_element_type=jnp.float32
        ).reshape(rows, key_heads * HD)
        * scale
    )
    query_grad = (
        jnp.einsum(
            "kgqs,skd->qkgd", dscores_b, key_split, preferred_element_type=jnp.float32
        ).reshape(rows, -1)
        * scale
    )
    return (query_grad, key_grad, value_grad)


def guarded(
    active,
    query_block,
    grad_block,
    sums_block,
    delta_block,
    key_block,
    value_block,
    query_index,
    key_index,
):
    rows = query_block.shape[0]

    def compute():
        return tile_terms(
            query_block,
            grad_block,
            sums_block,
            delta_block,
            key_block,
            value_block,
            query_index,
            key_index,
        )

    def nothing():
        return (
            jnp.zeros((rows, query_block.shape[1]), jnp.float32),
            jnp.zeros((rows, key_block.shape[1]), jnp.float32),
            jnp.zeros((rows, key_block.shape[1]), jnp.float32),
        )

    return lax.cond(active, compute, nothing)


def per_device(queries, out_grads, log_sums, deltas, keys, values, doc_ids):
    blocks = lax.axis_size("ctx")
    mine = lax.axis_index("ctx")
    ids = doc_ids[0]
    order = jnp.arange(blocks, dtype=jnp.int32)
    first = jnp.min(jnp.where(ids[:, None] == ids[None, :], order[None, :], blocks), axis=1)
    query_here = queries[0]
    grad_here = out_grads[0]
    sums_here = log_sums[0]
    delta_here = deltas[0]
    start_terms = guarded(
        first[mine] <= mine, query_here, grad_here, sums_here, delta_here, keys, values, mine, mine
    )

    def advance(step, carry):
        pair, partial_value, query_grad = carry
        pair = shifted((pair[0], pair[1]), "ctx", 1)
        partial_value = from_behind((partial_value[0], partial_value[1]), "ctx", 1)
        source = mine - step
        active = source >= first[mine]
        terms = guarded(
            active, query_here, grad_here, sums_here, delta_here, pair[0], pair[1], mine, source
        )
        return (
            pair,
            (partial_value[0] + terms[1], partial_value[1] + terms[2]),
            query_grad + terms[0],
        )

    carry = ((keys, values), (start_terms[1], start_terms[2]), start_terms[0])
    pair, partial_value, query_grad = lax.fori_loop(1, MAXSPAN, advance, carry)
    key_part, value_part = from_behind((partial_value[0], partial_value[1]), "ctx", 1 - MAXSPAN)
    summed = sent_together((key_part, value_part), "rec", 0, 1)
    return (
        query_grad[None].astype(jnp.bfloat16),
        summed[0].astype(jnp.bfloat16),
        summed[1].astype(jnp.bfloat16),
    )


def solution(mesh):
    return jax.shard_map(
        per_device,
        mesh=mesh,
        in_specs=(
            P("rec", "ctx", None),
            P("rec", "ctx", None),
            P("rec", None, "ctx"),
            P("rec", None, "ctx"),
            P("ctx", None),
            P("ctx", None),
            P("rec", None),
        ),
        out_specs=(P("rec", "ctx", None), P(("ctx", "rec"), None), P(("ctx", "rec"), None)),
        check_vma=False,
    )
```

profile of v0, /device:TPU:1, one launch (start us, length us, event | category | flops | bytes accessed | tf_op | source)
XLA Modules:
  0.0 126.4 jit_solution(2066228829599383198)
XLA Ops:
  0.6 1.6 %copy.141 = bf16[128,256]{1,0:T(8,128)(2,1)} copy(bf16[128,256]{1,0:T(8,128)(2,1)} %param.18) | data formatting | bytes 131072
  2.2 0.9 select_reduce_fusion
  3.1 0.6 dynamic_slice.10
  4.2 1.6 %copy.71 = bf16[128,256]{0,1:T(8,128)(2,1)} copy(bf16[128,256]{1,0:T(8,128)(2,1)} %param.17) | data formatting | bytes 131072 | tf_op jit(solution)/shard_map/while | solution.py:151
  5.8 1.6 %copy.72 = bf16[1,128,4096]{1,2,0:T(8,128)(2,1)S(1)} copy(bf16[1,128,4096]{2,1,0:T(8,128)(2,1)} %param.13) | data formatting | bytes 2097152 | tf_op jit(solution)/shard_map/while | solution.py:151
  7.4 1.3 %copy.73 = bf16[1,128,4096]{1,2,0:T(8,128)(2,1)} copy(bf16[1,128,4096]{2,1,0:T(8,128)(2,1)S(1)} %copy-done.1) | data formatting | bytes 2097152 | tf_op jit(solution)/shard_map/while | solution.py:151
  8.8 9.1 %conditional.2 = (f32[128,4096]{0,1:T(8,128)}, f32[128,256]{0,1:T(8,128)}, f32[128,256]{0,1:T(8,128)}) conditional(s32[]{:T(128)} %convert_element_type.32, () %tuple.45, (s32[]{:T(128)}, bf16[128,256]{1,0:T(8,128)(2,1)S(1)}, bf16[1,128,4096]{2,1,0:T(8,128)(2,1)}, f32[1,32,128]{2,1,0:T(8,128)S(1)}, bf16[128,256]{1,0:T(8,128)(2,1)}, ...), branch_computations={%region_1.2_spmd, %region_2.3_spmd} | conditional | flops 675332224 | bytes 20710440 | solution.py:118
  8.9 0.9 reshape.55
  9.8 0.7 copy.70
  10.5 1.6 %copy.69 = bf16[1,128,4096]{1,2,0:T(8,128)(2,1)S(1)} copy(bf16[1,128,4096]{2,1,0:T(8,128)(2,1)} %get-tuple-element.381) | data formatting | bytes 2097152 | tf_op jit(solution)/shard_map
  12.1 0.6 fusion.3
  12.7 1.1 fusion.5
  13.8 1.2 fusion.1
  15.0 1.1 fusion.4
  16.1 1.8 %convolution_multiply_fusion = f32[2,16,128,128]{2,3,1,0:T(8,128)} fusion(bf16[128,2,128,1]{0,2,3,1:T(8,128)(2,1)S(1)} %bitcast.127, bf16[2,16,128,128]{2,3,1,0:T(8,128)(2,1)S(1)} %fusion.1), kind=kOutput, calls=%fused_computation.6 | convolution fusion | flops 134742016 | bytes 3211264 | tf_op jit(solution)/shard_map/cond/branch_1_fun/kgqs,skd->qkgd/dot_general | solution.py:78
  17.8 74.0 %while.23 = (s32[]{:T(128)}, bf16[128,256]{0,1:T(8,128)(2,1)}, bf16[128,256]{1,0:T(8,128)(2,1)}, f32[128,256]{0,1:T(8,128)}, f32[128,256]{0,1:T(8,128)}, /*index...) while((s32[]{:T(128)}, bf16[128,256]{0,1:T(8,128)(2,1)}, ...), condition=%wide.region_6.7_spmd, body=%wide.region_3.6_spmd.sunk | while | flops 675922176 | bytes 29493708 | solution.py:151
  17.8 5.4 %collective-permute-start.2 = (f32[128,256]{0,1:T(8,128)}, f32[128,256]{0,1:T(8,128)}, u32[]{:S(2)}, u32[]{:S(2)}) collective-permute-start(f32[128,256]{0,1:T(8,128)} %get-tuple-element.533), channel_id=1, source_target_pairs={{0,4},{4,8},{8,12},{12,16},{16,20},{20,24},{24,28},{28,32},{32,36}... | collective-permute-start | bytes 393224 | tf_op jit(solution)/shard_map/while/body/eval_jaxpr/ppermute | solution.py:18
  23.2 1.9 %collective-permute-start.3 = (f32[128,256]{0,1:T(8,128)}, f32[128,256]{0,1:T(8,128)}, u32[]{:S(2)}, u32[]{:S(2)}) collective-permute-start(f32[128,256]{0,1:T(8,128)} %get-tuple-element.534), channel_id=1, source_target_pairs={{0,4},{4,8},{8,12},{12,16},{16,20},{20,24},{24,28},{28,32},{32,36}... | collective-permute-start | bytes 393224 | tf_op jit(solution)/shard_map/while/body/eval_jaxpr/ppermute | solution.py:18
  25.1 4.4 %collective-permute-start.1 = (bf16[128,256]{1,0:T(8,128)(2,1)}, bf16[128,256]{1,0:T(8,128)(2,1)S(1)}, u32[]{:S(2)}, u32[]{:S(2)}) collective-permute-start(bf16[128,256]{1,0:T(8,128)(2,1)} %get-tuple-element.532), channel_id=1, source_target_pairs={{0,4},{4,8},{8,12},{12,16},{16,20},{20,24},{24,28},{28,32},{32,36}... | collective-permute-start | bytes 196616 | tf_op jit(solution)/shard_map/while/body/eval_jaxpr/ppermute | solution.py:13
  29.5 1.9 %collective-permute-start = (bf16[128,256]{0,1:T(8,128)(2,1)}, bf16[128,256]{0,1:T(8,128)(2,1)S(1)}, u32[]{:S(2)}, u32[]{:S(2)}) collective-permute-start(bf16[128,256]{0,1:T(8,128)(2,1)} %get-tuple-element.531), channel_id=1, source_target_pairs={{0,4},{4,8},{8,12},{12,16},{16,20},{20,24},{24,28},{28,32},{32,36}... | collective-permute-start | bytes 196616 | tf_op jit(solution)/shard_map/while/body/eval_jaxpr/ppermute | solution.py:13
  32.0 1.1 collective-permute-done
  33.1 3.7 %conditional.4 = (f32[128,4096]{0,1:T(8,128)S(1)}, f32[128,256]{0,1:T(8,128)S(1)}, f32[128,256]{0,1:T(8,128)S(1)}) conditional(s32[]{:T(128)} %convert_element_type.43, () %tuple.67, (s32[]{:T(128)}, s32[]{:T(128)}, bf16[128,256]{0,1:T(8,128)(2,1)S(1)}, bf16[1,128,4096]{1,2,0:T(8,128)(2,1)S(1)}, f32[1,32,128]{2,1,0:T(8,128)S(1)}, ...), branch_computations={%region_4.4_spmd, %region_5.5_spmd} | conditional | flops 675332352 | bytes 20580436 | solution.py:118
  33.2 0.6 fusion.11
  33.8 0.5 copy-done
  34.3 0.4 fusion.13
  34.8 1.2 fusion.9
  35.9 0.4 fusion.12
  36.4 0.4 convolution_multiply_fusion.1
  36.8 3.1 %add.106 = f32[128,4096]{0,1:T(8,128)} add(f32[128,4096]{0,1:T(8,128)} %get-tuple-element.535, f32[128,4096]{0,1:T(8,128)S(1)} %get-tuple-element.504) | non-fusion elementwise | flops 524288 | bytes 6291456 | tf_op jit(solution)/shard_map/while/body/eval_jaxpr/add | solution.py:147
  39.9 0.6 copy.135
  40.5 0.6 copy.134
  41.2 1.6 %add.104 = f32[128,256]{0,1:T(8,128)} add(f32[128,256]{0,1:T(8,128)} %collective-permute-done.2, f32[128,256]{0,1:T(8,128)S(1)} %get-tuple-element.502) | non-fusion elementwise | flops 32768 | bytes 393216 | tf_op jit(solution)/shard_map/while/body/eval_jaxpr/add | solution.py:146
  42.7 1.6 %add.105 = f32[128,256]{0,1:T(8,128)} add(f32[128,256]{0,1:T(8,128)} %collective-permute-done.3, f32[128,256]{0,1:T(8,128)S(1)} %get-tuple-element.503) | non-fusion elementwise | flops 32768 | bytes 393216 | tf_op jit(solution)/shard_map/while/body/eval_jaxpr/add | solution.py:146
  44.3 1.9 %collective-permute-start.2 = (f32[128,256]{0,1:T(8,128)}, f32[128,256]{0,1:T(8,128)}, u32[]{:S(2)}, u32[]{:S(2)}) collective-permute-start(f32[128,256]{0,1:T(8,128)} %get-tuple-element.533), channel_id=1, source_target_pairs={{0,4},{4,8},{8,12},{12,16},{16,20},{20,24},{24,28},{28,32},{32,36}... | collective-permute-start | bytes 393224 | tf_op jit(solution)/shard_map/while/body/eval_jaxpr/ppermute | solution.py:18
  46.2 4.4 %collective-permute-start.3 = (f32[128,256]{0,1:T(8,128)}, f32[128,256]{0,1:T(8,128)}, u32[]{:S(2)}, u32[]{:S(2)}) collective-permute-start(f32[128,256]{0,1:T(8,128)} %get-tuple-element.534), channel_id=1, source_target_pairs={{0,4},{4,8},{8,12},{12,16},{16,20},{20,24},{24,28},{28,32},{32,36}... | collective-permute-start | bytes 393224 | tf_op jit(solution)/shard_map/while/body/eval_jaxpr/ppermute | solution.py:18
  50.6 5.1 %collective-permute-start.1 = (bf16[128,256]{1,0:T(8,128)(2,1)}, bf16[128,256]{1,0:T(8,128)(2,1)S(1)}, u32[]{:S(2)}, u32[]{:S(2)}) collective-permute-start(bf16[128,256]{1,0:T(8,128)(2,1)} %get-tuple-element.532), channel_id=1, source_target_pairs={{0,4},{4,8},{8,12},{12,16},{16,20},{20,24},{24,28},{28,32},{32,36}... | collective-permute-start | bytes 196616 | tf_op jit(solution)/shard_map/while/body/eval_jaxpr/ppermute | solution.py:13
  55.7 2.5 %collective-permute-start = (bf16[128,256]{0,1:T(8,128)(2,1)}, bf16[128,256]{0,1:T(8,128)(2,1)S(1)}, u32[]{:S(2)}, u32[]{:S(2)}) collective-permute-start(bf16[128,256]{0,1:T(8,128)(2,1)} %get-tuple-element.531), channel_id=1, source_target_pairs={{0,4},{4,8},{8,12},{12,16},{16,20},{20,24},{24,28},{28,32},{32,36}... | collective-permute-start | bytes 196616 | tf_op jit(solution)/shard_map/while/body/eval_jaxpr/ppermute | solution.py:13
  58.7 1.1 collective-permute-done
  60.0 3.1 %add.106 = f32[128,4096]{0,1:T(8,128)} add(f32[128,4096]{0,1:T(8,128)} %get-tuple-element.535, f32[128,4096]{0,1:T(8,128)S(1)} %get-tuple-element.504) | non-fusion elementwise | flops 524288 | bytes 6291456 | tf_op jit(solution)/shard_map/while/body/eval_jaxpr/add | solution.py:147
  63.1 0.6 copy.135
  63.7 0.6 copy.134
  64.3 1.6 %add.104 = f32[128,256]{0,1:T(8,128)} add(f32[128,256]{0,1:T(8,128)} %collective-permute-done.2, f32[128,256]{0,1:T(8,128)S(1)} %get-tuple-element.502) | non-fusion elementwise | flops 32768 | bytes 393216 | tf_op jit(solution)/shard_map/while/body/eval_jaxpr/add | solution.py:146
  65.9 1.6 %add.105 = f32[128,256]{0,1:T(8,128)} add(f32[128,256]{0,1:T(8,128)} %collective-permute-done.3, f32[128,256]{0,1:T(8,128)S(1)} %get-tuple-element.503) | non-fusion elementwise | flops 32768 | bytes 393216 | tf_op jit(solution)/shard_map/while/body/eval_jaxpr/add | solution.py:146
  67.5 4.2 %collective-permute-start.2 = (f32[128,256]{0,1:T(8,128)}, f32[128,256]{0,1:T(8,128)}, u32[]{:S(2)}, u32[]{:S(2)}) collective-permute-start(f32[128,256]{0,1:T(8,128)} %get-tuple-element.533), channel_id=1, source_target_pairs={{0,4},{4,8},{8,12},{12,16},{16,20},{20,24},{24,28},{28,32},{32,36}... | collective-permute-start | bytes 393224 | tf_op jit(solution)/shard_map/while/body/eval_jaxpr/ppermute | solution.py:18
  71.6 1.9 %collective-permute-start.3 = (f32[128,256]{0,1:T(8,128)}, f32[128,256]{0,1:T(8,128)}, u32[]{:S(2)}, u32[]{:S(2)}) collective-permute-start(f32[128,256]{0,1:T(8,128)} %get-tuple-element.534), channel_id=1, source_target_pairs={{0,4},{4,8},{8,12},{12,16},{16,20},{20,24},{24,28},{28,32},{32,36}... | collective-permute-start | bytes 393224 | tf_op jit(solution)/shard_map/while/body/eval_jaxpr/ppermute | solution.py:18
  73.5 7.0 %collective-permute-start.1 = (bf16[128,256]{1,0:T(8,128)(2,1)}, bf16[128,256]{1,0:T(8,128)(2,1)S(1)}, u32[]{:S(2)}, u32[]{:S(2)}) collective-permute-start(bf16[128,256]{1,0:T(8,128)(2,1)} %get-tuple-element.532), channel_id=1, source_target_pairs={{0,4},{4,8},{8,12},{12,16},{16,20},{20,24},{24,28},{28,32},{32,36}... | collective-permute-start | bytes 196616 | tf_op jit(solution)/shard_map/while/body/eval_jaxpr/ppermute | solution.py:13
  80.5 1.9 %collective-permute-start = (bf16[128,256]{0,1:T(8,128)(2,1)}, bf16[128,256]{0,1:T(8,128)(2,1)S(1)}, u32[]{:S(2)}, u32[]{:S(2)}) collective-permute-start(bf16[128,256]{0,1:T(8,128)(2,1)} %get-tuple-element.531), channel_id=1, source_target_pairs={{0,4},{4,8},{8,12},{12,16},{16,20},{20,24},{24,28},{28,32},{32,36}... | collective-permute-start | bytes 196616 | tf_op jit(solution)/shard_map/while/body/eval_jaxpr/ppermute | solution.py:13
  83.0 1.1 collective-permute-done
  84.3 3.1 %add.106 = f32[128,4096]{0,1:T(8,128)} add(f32[128,4096]{0,1:T(8,128)} %get-tuple-element.535, f32[128,4096]{0,1:T(8,128)S(1)} %get-tuple-element.504) | non-fusion elementwise | flops 524288 | bytes 6291456 | tf_op jit(solution)/shard_map/while/body/eval_jaxpr/add | solution.py:147
  87.4 0.6 copy.135
  88.0 0.6 copy.134
  88.7 1.6 %add.104 = f32[128,256]{0,1:T(8,128)} add(f32[128,256]{0,1:T(8,128)} %collective-permute-done.2, f32[128,256]{0,1:T(8,128)S(1)} %get-tuple-element.502) | non-fusion elementwise | flops 32768 | bytes 393216 | tf_op jit(solution)/shard_map/while/body/eval_jaxpr/add | solution.py:146
  90.2 1.6 %add.105 = f32[128,256]{0,1:T(8,128)} add(f32[128,256]{0,1:T(8,128)} %collective-permute-done.3, f32[128,256]{0,1:T(8,128)S(1)} %get-tuple-element.503) | non-fusion elementwise | flops 32768 | bytes 393216 | tf_op jit(solution)/shard_map/while/body/eval_jaxpr/add | solution.py:146
  91.8 1.0 copy.76
  92.8 3.7 %collective-permute-start.5 = (f32[128,256]{1,0:T(8,128)S(1)}, f32[128,256]{1,0:T(8,128)S(1)}, u32[]{:S(2)}, u32[]{:S(2)}) collective-permute-start(f32[128,256]{1,0:T(8,128)S(1)} %copy.76), channel_id=1, source_target_pairs={{0,500},{4,504},{8,508},{12,0},{16,4},{20,8},{24,12},{28,16},{32,2... | collective-permute-start | bytes 393224 | tf_op jit(solution)/shard_map/ppermute | solution.py:18
  96.5 1.0 copy.75
  97.5 3.0 %collective-permute-start.4 = (f32[128,256]{1,0:T(8,128)S(1)}, f32[128,256]{1,0:T(8,128)S(1)}, u32[]{:S(2)}, u32[]{:S(2)}) collective-permute-start(f32[128,256]{1,0:T(8,128)S(1)} %copy.75), channel_id=1, source_target_pairs={{0,500},{4,504},{8,508},{12,0},{16,4},{20,8},{24,12},{28,16},{32,2... | collective-permute-start | bytes 393224 | tf_op jit(solution)/shard_map/ppermute | solution.py:18
  100.5 1.7 %collective-permute-done.5 = f32[128,256]{1,0:T(8,128)S(1)} collective-permute-done((f32[128,256]{1,0:T(8,128)S(1)}, f32[128,256]{1,0:T(8,128)S(1)}, u32[]{:S(2)}, u32[]{:S(2)}) %collective-permute-start.5) | collective-permute-done | bytes 131104 | tf_op jit(solution)/shard_map/ppermute | solution.py:18
  102.2 4.7 %collective-permute-done.4 = f32[128,256]{1,0:T(8,128)S(1)} collective-permute-done((f32[128,256]{1,0:T(8,128)S(1)}, f32[128,256]{1,0:T(8,128)S(1)}, u32[]{:S(2)}, u32[]{:S(2)}) %collective-permute-start.4) | collective-permute-done | bytes 131104 | tf_op jit(solution)/shard_map/ppermute | solution.py:18
  106.9 0.7 pad_maximum_fusion
  107.6 8.8 %all-to-all-start = ((f32[4,32,512]{2,1,0:T(8,128)}), f32[4,32,512]{2,1,0:T(8,128)S(1)}, u32[]{:S(2)}, u32[]{:S(2)}) async-start(f32[4,32,512]{2,1,0:T(8,128)} %bitcast.46), calls=%async_computation | async-start | bytes 524288 | tf_op jit(solution)/shard_map/all_to_all | solution.py:29
  116.4 2.5 %copy.74 = bf16[128,4096]{1,0:T(8,128)(2,1)} copy(f32[128,4096]{0,1:T(8,128)} %get-tuple-element.338) | data formatting | bytes 3145728 | tf_op jit(solution)/shard_map/while | solution.py:151
  118.9 6.8 %all-to-all-done = f32[4,32,512]{2,1,0:T(8,128)S(1)} async-done(((f32[4,32,512]{2,1,0:T(8,128)}), f32[4,32,512]{2,1,0:T(8,128)S(1)}, u32[]{:S(2)}, u32[]{:S(2)}) %all-to-all-start) | async-done | bytes 262176 | tf_op jit(solution)/shard_map/all_to_all | solution.py:29
  125.8 0.6 fusion.16
  (31 shorter events, 1.0 us)
Async XLA Ops:
  0.6 6.8 %copy-start.1 = (bf16[1,128,4096]{2,1,0:T(8,128)(2,1)S(1)}, bf16[1,128,4096]{2,1,0:T(8,128)(2,1)}, u32[]{:S(2)}) copy-start(bf16[1,128,4096]{2,1,0:T(8,128)(2,1)} %param.14) | copy-start | bytes 3145732
  5.8 3.0 %copy-start.2 = (f32[1,32,128]{2,1,0:T(8,128)S(1)}, f32[1,32,128]{2,1,0:T(8,128)}, u32[]{:S(2)}) copy-start(f32[1,32,128]{2,1,0:T(8,128)} %param.15) | copy-start | bytes 49156
  5.8 3.0 %copy-start.3 = (bf16[128,256]{1,0:T(8,128)(2,1)S(1)}, bf16[128,256]{1,0:T(8,128)(2,1)}, u32[]{:S(2)}) copy-start(bf16[128,256]{1,0:T(8,128)(2,1)} %param.17) | copy-start | bytes 196612
  17.8 23.3 %collective-permute-start.2 = (f32[128,256]{0,1:T(8,128)}, f32[128,256]{0,1:T(8,128)}, u32[]{:S(2)}, u32[]{:S(2)}) collective-permute-start(f32[128,256]{0,1:T(8,128)} %get-tuple-element.533), channel_id=1, source_target_pairs={{0,4},{4,8},{8,12},{12,16},{16,20},{20,24},{24,28},{28,32},{32,36}... | collective-permute-start | bytes 393224 | tf_op jit(solution)/shard_map/while/body/eval_jaxpr/ppermute | solution.py:18
  23.2 19.5 %collective-permute-start.3 = (f32[128,256]{0,1:T(8,128)}, f32[128,256]{0,1:T(8,128)}, u32[]{:S(2)}, u32[]{:S(2)}) collective-permute-start(f32[128,256]{0,1:T(8,128)} %get-tuple-element.534), channel_id=1, source_target_pairs={{0,4},{4,8},{8,12},{12,16},{16,20},{20,24},{24,28},{28,32},{32,36}... | collective-permute-start | bytes 393224 | tf_op jit(solution)/shard_map/while/body/eval_jaxpr/ppermute | solution.py:18
  25.1 6.9 %collective-permute-start.1 = (bf16[128,256]{1,0:T(8,128)(2,1)}, bf16[128,256]{1,0:T(8,128)(2,1)S(1)}, u32[]{:S(2)}, u32[]{:S(2)}) collective-permute-start(bf16[128,256]{1,0:T(8,128)(2,1)} %get-tuple-element.532), channel_id=1, source_target_pairs={{0,4},{4,8},{8,12},{12,16},{16,20},{20,24},{24,28},{28,32},{32,36}... | collective-permute-start | bytes 196616 | tf_op jit(solution)/shard_map/while/body/eval_jaxpr/ppermute | solution.py:13
  29.5 3.6 %collective-permute-start = (bf16[128,256]{0,1:T(8,128)(2,1)}, bf16[128,256]{0,1:T(8,128)(2,1)S(1)}, u32[]{:S(2)}, u32[]{:S(2)}) collective-permute-start(bf16[128,256]{0,1:T(8,128)(2,1)} %get-tuple-element.531), channel_id=1, source_target_pairs={{0,4},{4,8},{8,12},{12,16},{16,20},{20,24},{24,28},{28,32},{32,36}... | collective-permute-start | bytes 196616 | tf_op jit(solution)/shard_map/while/body/eval_jaxpr/ppermute | solution.py:13
  33.1 1.2 copy-start
  44.3 20.0 %collective-permute-start.2 = (f32[128,256]{0,1:T(8,128)}, f32[128,256]{0,1:T(8,128)}, u32[]{:S(2)}, u32[]{:S(2)}) collective-permute-start(f32[128,256]{0,1:T(8,128)} %get-tuple-element.533), channel_id=1, source_target_pairs={{0,4},{4,8},{8,12},{12,16},{16,20},{20,24},{24,28},{28,32},{32,36}... | collective-permute-start | bytes 393224 | tf_op jit(solution)/shard_map/while/body/eval_jaxpr/ppermute | solution.py:18
  46.2 19.7 %collective-permute-start.3 = (f32[128,256]{0,1:T(8,128)}, f32[128,256]{0,1:T(8,128)}, u32[]{:S(2)}, u32[]{:S(2)}) collective-permute-start(f32[128,256]{0,1:T(8,128)} %get-tuple-element.534), channel_id=1, source_target_pairs={{0,4},{4,8},{8,12},{12,16},{16,20},{20,24},{24,28},{28,32},{32,36}... | collective-permute-start | bytes 393224 | tf_op jit(solution)/shard_map/while/body/eval_jaxpr/ppermute | solution.py:18
  50.6 8.1 %collective-permute-start.1 = (bf16[128,256]{1,0:T(8,128)(2,1)}, bf16[128,256]{1,0:T(8,128)(2,1)S(1)}, u32[]{:S(2)}, u32[]{:S(2)}) collective-permute-start(bf16[128,256]{1,0:T(8,128)(2,1)} %get-tuple-element.532), channel_id=1, source_target_pairs={{0,4},{4,8},{8,12},{12,16},{16,20},{20,24},{24,28},{28,32},{32,36}... | collective-permute-start | bytes 196616 | tf_op jit(solution)/shard_map/while/body/eval_jaxpr/ppermute | solution.py:13
  55.7 4.1 %collective-permute-start = (bf16[128,256]{0,1:T(8,128)(2,1)}, bf16[128,256]{0,1:T(8,128)(2,1)S(1)}, u32[]{:S(2)}, u32[]{:S(2)}) collective-permute-start(bf16[128,256]{0,1:T(8,128)(2,1)} %get-tuple-element.531), channel_id=1, source_target_pairs={{0,4},{4,8},{8,12},{12,16},{16,20},{20,24},{24,28},{28,32},{32,36}... | collective-permute-start | bytes 196616 | tf_op jit(solution)/shard_map/while/body/eval_jaxpr/ppermute | solution.py:13
  67.5 21.2 %collective-permute-start.2 = (f32[128,256]{0,1:T(8,128)}, f32[128,256]{0,1:T(8,128)}, u32[]{:S(2)}, u32[]{:S(2)}) collective-permute-start(f32[128,256]{0,1:T(8,128)} %get-tuple-element.533), channel_id=1, source_target_pairs={{0,4},{4,8},{8,12},{12,16},{16,20},{20,24},{24,28},{28,32},{32,36}... | collective-permute-start | bytes 393224 | tf_op jit(solution)/shard_map/while/body/eval_jaxpr/ppermute | solution.py:18
  71.6 18.6 %collective-permute-start.3 = (f32[128,256]{0,1:T(8,128)}, f32[128,256]{0,1:T(8,128)}, u32[]{:S(2)}, u32[]{:S(2)}) collective-permute-start(f32[128,256]{0,1:T(8,128)} %get-tuple-element.534), channel_id=1, source_target_pairs={{0,4},{4,8},{8,12},{12,16},{16,20},{20,24},{24,28},{28,32},{32,36}... | collective-permute-start | bytes 393224 | tf_op jit(solution)/shard_map/while/body/eval_jaxpr/ppermute | solution.py:18
  73.5 9.5 %collective-permute-start.1 = (bf16[128,256]{1,0:T(8,128)(2,1)}, bf16[128,256]{1,0:T(8,128)(2,1)S(1)}, u32[]{:S(2)}, u32[]{:S(2)}) collective-permute-start(bf16[128,256]{1,0:T(8,128)(2,1)} %get-tuple-element.532), channel_id=1, source_target_pairs={{0,4},{4,8},{8,12},{12,16},{16,20},{20,24},{24,28},{28,32},{32,36}... | collective-permute-start | bytes 196616 | tf_op jit(solution)/shard_map/while/body/eval_jaxpr/ppermute | solution.py:13
  80.5 3.6 %collective-permute-start = (bf16[128,256]{0,1:T(8,128)(2,1)}, bf16[128,256]{0,1:T(8,128)(2,1)S(1)}, u32[]{:S(2)}, u32[]{:S(2)}) collective-permute-start(bf16[128,256]{0,1:T(8,128)(2,1)} %get-tuple-element.531), channel_id=1, source_target_pairs={{0,4},{4,8},{8,12},{12,16},{16,20},{20,24},{24,28},{28,32},{32,36}... | collective-permute-start | bytes 196616 | tf_op jit(solution)/shard_map/while/body/eval_jaxpr/ppermute | solution.py:13
  92.8 9.4 %collective-permute-start.5 = (f32[128,256]{1,0:T(8,128)S(1)}, f32[128,256]{1,0:T(8,128)S(1)}, u32[]{:S(2)}, u32[]{:S(2)}) collective-permute-start(f32[128,256]{1,0:T(8,128)S(1)} %copy.76), channel_id=1, source_target_pairs={{0,500},{4,504},{8,508},{12,0},{16,4},{20,8},{24,12},{28,16},{32,2... | collective-permute-start | bytes 393224 | tf_op jit(solution)/shard_map/ppermute | solution.py:18
  97.5 9.4 %collective-permute-start.4 = (f32[128,256]{1,0:T(8,128)S(1)}, f32[128,256]{1,0:T(8,128)S(1)}, u32[]{:S(2)}, u32[]{:S(2)}) collective-permute-start(f32[128,256]{1,0:T(8,128)S(1)} %copy.75), channel_id=1, source_target_pairs={{0,500},{4,504},{8,508},{12,0},{16,4},{20,8},{24,12},{28,16},{32,2... | collective-permute-start | bytes 393224 | tf_op jit(solution)/shard_map/ppermute | solution.py:18
  107.6 18.1 %all-to-all-start = ((f32[4,32,512]{2,1,0:T(8,128)}), f32[4,32,512]{2,1,0:T(8,128)S(1)}, u32[]{:S(2)}, u32[]{:S(2)}) async-start(f32[4,32,512]{2,1,0:T(8,128)} %bitcast.46), calls=%async_computation | async-start | bytes 524288 | tf_op jit(solution)/shard_map/all_to_all | solution.py:29
where the time goes:
time: 128 us; the launch traced here: 126 us
  starting transfers between devices  57.8 us (45%)
  other arithmetic  20.6 us (16%)
  local copies, waits for them, and re-layouts  19.6 us (15%)
  waiting for transfers between devices  16.4 us (13%)
  matrix products  8.73 us (7%)
  loops' own time  1.94 us (2%)
    ppermute x8, starting transfers between devices, from_behind(): lax.ppermute(shard, axis, [(i, (i + by) % peers) for i in range(peers)])  26.3 us
    ppermute x6, starting transfers between devices, shifted(): return lax.ppermute(block, axis, route)  22.7 us
    add x3, other arithmetic, advance(): query_grad + terms[0]  9.39 us
    while x6, local copies, waits for them, and re-layouts, per_device(): pair, partial_value, query_grad = lax.fori_loop(1, MAXSPAN, advance, carry)  9.05 us
    all_to_all x1, starting transfers between devices, summed_on_arrival(): lax.all_to_all(pieces, axis, split_axis=0, concat_axis=0, tiled=True)  8.78 us
    all_to_all x1, waiting for transfers between devices, summed_on_arrival(): lax.all_to_all(pieces, axis, split_axis=0, concat_axis=0, tiled=True)  6.8 us
    ppermute x8, waiting for transfers between devices, from_behind(): lax.ppermute(shard, axis, [(i, (i + by) % peers) for i in range(peers)])  6.44 us
    add x3, other arithmetic, advance(): partial_value[1] + terms[2]  4.7 us
  transfers between devices with their start and end apart: 15, of which 6 were waited for; matrix products, arithmetic and copies ran while one was open for 20% of the time, Pallas kernels for 0%

commit v1 on v0

v1 whole, which is shorter than its diff:
```python
import math

import jax
import jax.numpy as jnp
from jax import lax
from jax.experimental import pallas as pl
from jax.experimental.pallas import tpu as pltpu
from jax.sharding import PartitionSpec as P

HD = 128
TOK = 128
SPAN = 4
HEADS = 32
GROUP = 16
TOGETHER = 4
SCALE = HD**-0.5
LOG2E = math.log2(math.e)
FAR = 1e30


def dot_nt(a, b):
    return lax.dot_general(a, b, (((1,), (1,)), ((), ())), preferred_element_type=jnp.float32)


def dot_nn(a, b):
    return lax.dot_general(a, b, (((1,), (0,)), ((), ())), preferred_element_type=jnp.float32)


def attention_kernel(
    ids, q_ref, o_ref, lse_ref, delta_ref, k_ref, v_ref, r1, r2, r3,
    dq_ref, keep_ref, send_ref, ks, vs, kts, dk, dv,
):
    me = lax.axis_index("ctx")
    away = [jnp.float32(0.0)]
    for back in range(1, SPAN):
        at = jnp.maximum(me - back, 0)
        live = jnp.logical_and(me >= back, ids[0, at] == ids[0, me])
        away.append(jnp.where(live, jnp.float32(0.0), jnp.float32(FAR)))
    for g in range(2):
        cols = slice(g * HD, (g + 1) * HD)
        later = slice((g + 2) * HD, (g + 3) * HD)
        for back in range(SPAN):
            at = slice(back * TOK, (back + 1) * TOK)
            got = (None, r1, r2, r3)[back]
            kb = k_ref[:, cols] if back == 0 else got[:, cols]
            vb = v_ref[:, cols] if back == 0 else got[:, later]
            ks[g, at, :] = kb
            vs[g, at, :] = vb
            kts[g, :, at] = kb.T
    dk[...] = jnp.zeros_like(dk)
    dv[...] = jnp.zeros_like(dv)
    key_at = lax.broadcasted_iota(jnp.int32, (TOK, TOK), 0)
    causal = key_at <= lax.broadcasted_iota(jnp.int32, (TOK, TOK), 1)
    for g in range(2):

        def step(i, carry):
            head = g * GROUP + i * TOGETHER
            col = pl.multiple_of(head * HD, TOGETHER * HD)
            qs = q_ref[:, pl.ds(col, TOGETHER * HD)]
            os = o_ref[:, pl.ds(col, TOGETHER * HD)]
            q = jnp.concatenate([qs[:, j * HD : (j + 1) * HD] for j in range(TOGETHER)], 0)
            o = jnp.concatenate([os[:, j * HD : (j + 1) * HD] for j in range(TOGETHER)], 0)
            scores = dot_nt(ks[g], q)
            dprobs = dot_nt(vs[g], o)
            probs_b, dscores_b = [], []
            for j in range(TOGETHER):
                sums = lse_ref[pl.ds(head + j, 1), :] * LOG2E
                delta = delta_ref[pl.ds(head + j, 1), :]
                p_rows, d_rows = [], []
                for back in range(SPAN):
                    tile = (
                        slice(back * TOK, (back + 1) * TOK),
                        slice(j * TOK, (j + 1) * TOK),
                    )
                    p = jnp.exp2(scores[tile] * (SCALE * LOG2E) - (sums + away[back]))
                    if back == 0:
                        p = jnp.where(causal, p, 0.0)
                    p_rows.append(p.astype(jnp.bfloat16))
                    d_rows.append((p * (dprobs[tile] - delta)).astype(jnp.bfloat16))
                probs_b.append(jnp.concatenate(p_rows, 0))
                dscores_b.append(jnp.concatenate(d_rows, 0))
            probs_b = jnp.concatenate(probs_b, 1)
            dscores_b = jnp.concatenate(dscores_b, 1)
            dv[g] += dot_nn(probs_b, o)
            dk[g] += dot_nn(dscores_b, q)
            dqt = (dot_nn(kts[g], dscores_b) * SCALE).astype(jnp.bfloat16)
            for j in range(TOGETHER):
                at = pl.multiple_of(col + j * HD, HD)
                dq_ref[:, pl.ds(at, HD)] = dqt[:, j * TOK : (j + 1) * TOK].T
            return carry

        lax.fori_loop(0, GROUP // TOGETHER, step, 0)
    for g in range(2):
        cols = slice(g * HD, (g + 1) * HD)
        later = slice((g + 2) * HD, (g + 3) * HD)
        for back in range(SPAN):
            at = slice(back * TOK, (back + 1) * TOK)
            key_part = dk[g, at, :] * SCALE
            value_part = dv[g, at, :]
            if back == 0:
                keep_ref[:, cols] = key_part
                keep_ref[:, later] = value_part
            else:
                send_ref[back - 1, :, cols] = key_part.astype(jnp.bfloat16)
                send_ref[back - 1, :, later] = value_part.astype(jnp.bfloat16)


def attention(ids, q, o, lse, delta, k, v, r1, r2, r3):
    vmem = pl.BlockSpec(memory_space=pltpu.VMEM)
    width = 4 * HD
    return pl.pallas_call(
        attention_kernel,
        out_shape=(
            jax.ShapeDtypeStruct(q.shape, jnp.bfloat16),
            jax.ShapeDtypeStruct((TOK, width), jnp.float32),
            jax.ShapeDtypeStruct((SPAN - 1, TOK, width), jnp.bfloat16),
        ),
        in_specs=[pl.BlockSpec(memory_space=pltpu.SMEM)] + [vmem] * 9,
        out_specs=(vmem, vmem, vmem),
        scratch_shapes=[
            pltpu.VMEM((2, SPAN * TOK, HD), jnp.bfloat16),
            pltpu.VMEM((2, SPAN * TOK, HD), jnp.bfloat16),
            pltpu.VMEM((2, HD, SPAN * TOK), jnp.bfloat16),
            pltpu.VMEM((2, SPAN * TOK, HD), jnp.float32),
            pltpu.VMEM((2, SPAN * TOK, HD), jnp.float32),
        ],
        compiler_params=pltpu.CompilerParams(vmem_limit_bytes=24 << 20),
        cost_estimate=pl.CostEstimate(
            flops=10 * HEADS * SPAN * TOK * TOK * HD,
            bytes_accessed=5 << 20,
            transcendentals=HEADS * SPAN * TOK * TOK,
        ),
    )(ids, q, o, lse, delta, k, v, r1, r2, r3)


def shifted(block, by):
    devices = range(lax.axis_size("ctx"))
    return lax.ppermute(block, "ctx", [(i, i + by) for i in devices if i + by in devices])


def per_device(queries, out_grads, log_sums, deltas, keys, values, doc_ids):
    both = jnp.concatenate([keys, values], axis=1)
    behind = [shifted(both, by) for by in range(1, SPAN)]
    query_grad, total, parts = attention(
        doc_ids, queries[0], out_grads[0], log_sums[0], deltas[0], keys, values, *behind
    )
    for by in range(1, SPAN):
        total = total + shifted(parts[by - 1], -by).astype(jnp.float32)
    peers = lax.axis_size("rec")
    pieces = total.astype(jnp.bfloat16).reshape(peers, TOK // peers, -1)
    arrived = lax.all_to_all(pieces, "rec", 0, 0, tiled=True)
    summed = arrived.astype(jnp.float32).sum(axis=0).astype(jnp.bfloat16)
    return query_grad[None], summed[:, : 2 * HD], summed[:, 2 * HD :]


def solution(mesh):
    return jax.shard_map(
        per_device,
        mesh=mesh,
        in_specs=(
            P("rec", "ctx", None),
            P("rec", "ctx", None),
            P("rec", None, "ctx"),
            P("rec", None, "ctx"),
            P("ctx", None),
            P("ctx", None),
            P("rec", None),
        ),
        out_specs=(P("rec", "ctx", None), P(("ctx", "rec"), None), P(("ctx", "rec"), None)),
        check_vma=False,
    )
```

time: 128 us -> 65 us (0.51)
  the two profiles are of different devices: /device:TPU:1 before, /device:TPU:6 now
where the time goes in v1:
time: 65 us; the launch traced here: 64.6 us
  starting transfers between devices  21.3 us (33%)
  blocking collectives  15.1 us (23%)
  waiting for transfers between devices  13.9 us (21%)
  Pallas kernels  8.81 us (14%)
  local copies, waits for them, and re-layouts  4.64 us (7%)
  between operations  0.74 us (1%)
    ppermute x6, starting transfers between devices, shifted(): lax.ppermute(block, 'ctx', [(i, i + by) for i in devices if i + by in dev...  21.3 us
    all_to_all x1, blocking collectives, per_device(): arrived = lax.all_to_all(pieces, 'rec', 0, 0, tiled=True)  15.1 us
    ppermute x6, waiting for transfers between devices, shifted(): lax.ppermute(block, 'ctx', [(i, i + by) for i in devices if i + by in dev...  13.9 us
    pallas_call x1, Pallas kernels, attention(): pl.pallas_call(attention_kernel, out_shape=(jax.ShapeDtypeStruct(q.shape,...  8.81 us
    unnamed x15, local copies, waits for them, and re-layouts  3.99 us
  transfers between devices with their start and end apart: 6, of which 5 were waited for; matrix products, arithmetic and copies ran while one was open for 0% of the time, Pallas kernels for 0%

profile of v1, /device:TPU:6, one launch (start us, length us, event | category | flops | bytes accessed | tf_op | source)
XLA Modules:
  0.0 64.6 jit_solution(7339881069042116961)
XLA Ops:
  0.6 0.0 copy-start.1
  0.6 0.9 %constant_dynamic-update-slice_fusion.1 = bf16[128,512]{1,0:T(8,128)(2,1)S(1)} fusion(bf16[128,256]{1,0:T(8,128)(2,1)} %k_ref.1), kind=kLoop, calls=%fused_computation.5 | loop fusion | bytes 131072
  1.5 0.0 copy-done.1
  1.5 0.0 copy-start
  1.5 0.0 copy-start.4
  1.5 0.0 copy-start.5
  1.6 3.9 %collective-permute-start.2 = (bf16[128,512]{1,0:T(8,128)(2,1)S(1)}, bf16[128,512]{1,0:T(8,128)(2,1)S(1)}, u32[]{:S(2)}, u32[]{:S(2)}) collective-permute-start(bf16[128,512]{1,0:T(8,128)(2,1)S(1)} %constant_dynamic-update-slice_fusion), channel_id=1, source_target_pairs={{0,12},{4,16},{8,20},{12,24},{16,28},{20,32},{24,36},{28,40},{32,4... | collective-permute-start | bytes 393224 | tf_op jit(solution)/shard_map/ppermute | solution.py:138
  5.4 4.3 %collective-permute-start.1 = (bf16[128,512]{1,0:T(8,128)(2,1)S(1)}, bf16[128,512]{1,0:T(8,128)(2,1)S(1)}, u32[]{:S(2)}, u32[]{:S(2)}) collective-permute-start(bf16[128,512]{1,0:T(8,128)(2,1)S(1)} %constant_dynamic-update-slice_fusion), channel_id=1, source_target_pairs={{0,8},{4,12},{8,16},{12,20},{16,24},{20,28},{24,32},{28,36},{32,40... | collective-permute-start | bytes 393224 | tf_op jit(solution)/shard_map/ppermute | solution.py:138
  9.7 4.1 %collective-permute-start = (bf16[128,512]{1,0:T(8,128)(2,1)S(1)}, bf16[128,512]{1,0:T(8,128)(2,1)S(1)}, u32[]{:S(2)}, u32[]{:S(2)}) collective-permute-start(bf16[128,512]{1,0:T(8,128)(2,1)S(1)} %constant_dynamic-update-slice_fusion), channel_id=1, source_target_pairs={{0,4},{4,8},{8,12},{12,16},{16,20},{20,24},{24,28},{28,32},{32,36}... | collective-permute-start | bytes 393224 | tf_op jit(solution)/shard_map/ppermute | solution.py:138
  13.8 3.5 %collective-permute-done.2.r3 = bf16[128,512]{1,0:T(8,128)(2,1)S(1)} collective-permute-done((bf16[128,512]{1,0:T(8,128)(2,1)S(1)}, bf16[128,512]{1,0:T(8,128)(2,1)S(1)}, u32[]{:S(2)}, u32[]{:S(2)}) %collective-permute-start.2) | collective-permute-done | bytes 131104 | tf_op jit(solution)/shard_map/ppermute | solution.py:138
  17.3 5.1 %collective-permute-done.1.r2 = bf16[128,512]{1,0:T(8,128)(2,1)S(1)} collective-permute-done((bf16[128,512]{1,0:T(8,128)(2,1)S(1)}, bf16[128,512]{1,0:T(8,128)(2,1)S(1)}, u32[]{:S(2)}, u32[]{:S(2)}) %collective-permute-start.1) | collective-permute-done | bytes 131104 | tf_op jit(solution)/shard_map/ppermute | solution.py:138
  22.4 0.6 collective-permute-done.r1
  23.0 0.0 copy-start.6
  23.0 0.0 copy-done
  23.0 0.0 copy-done.4
  23.0 0.0 copy-done.5
  23.0 0.6 copy-done.6
  23.7 0.0 copy-start.2
  23.7 1.2 %copy-done.2 = bf16[1,128,4096]{2,1,0:T(8,128)(2,1)S(1)} copy-done((bf16[1,128,4096]{2,1,0:T(8,128)(2,1)S(1)}, bf16[1,128,4096]{2,1,0:T(8,128)(2,1)}, u32[]{:S(2)}) %copy-start.2) | copy-done | bytes 1048600
  24.9 0.0 copy-start.3
  24.9 1.2 %copy-done.3 = bf16[1,128,4096]{2,1,0:T(8,128)(2,1)S(1)} copy-done((bf16[1,128,4096]{2,1,0:T(8,128)(2,1)S(1)}, bf16[1,128,4096]{2,1,0:T(8,128)(2,1)}, u32[]{:S(2)}) %copy-start.3) | copy-done | bytes 1048600
  26.1 8.8 %shard_map.94 = (bf16[128,4096]{1,0:T(8,128)(2,1)}, f32[128,512]{1,0:T(8,128)S(1)}, bf16[3,128,512]{2,1,0:T(8,128)(2,1)S(1)}) custom-call(s32[1,128]{1,0:T(1,128)S(1)} %copy-done.6, bf16[128,4096]{1,0:T(8,128)(2,1)S(1)} %bitcast.12, bf16[128,4096]{1,0:T(8,128)(2,1)S(1)} %bitcast.13, f32[32,128]{1,0:T(8,128)S(1)} %bitcast.14, f32[32,128]{1,0:T(8,128)S(1)} %bitcast.15, ...), custom_call_target="tpu_custom_call" | custom-call | flops 2684354560 | bytes 5242880 | tf_op jit(solution)/shard_map/pallas_call | solution.py:111
  35.0 1.9 %collective-permute-start.3 = (bf16[128,512]{1,0:T(8,128)(2,1)S(1)}, bf16[128,512]{1,0:T(8,128)(2,1)S(1)}, u32[]{:S(2)}, u32[]{:S(2)}) collective-permute-start(bf16[128,512]{1,0:T(8,128)(2,1)S(1)} %get-tuple-element.9), channel_id=1, source_target_pairs={{4,0},{8,4},{12,8},{16,12},{20,16},{24,20},{28,24},{32,28},{36,32}... | collective-permute-start | bytes 393224 | tf_op jit(solution)/shard_map/ppermute | solution.py:138
  36.9 4.3 %collective-permute-start.5 = (bf16[128,512]{1,0:T(8,128)(2,1)S(1)}, bf16[128,512]{1,0:T(8,128)(2,1)S(1)}, u32[]{:S(2)}, u32[]{:S(2)}) collective-permute-start(bf16[128,512]{1,0:T(8,128)(2,1)S(1)} %get-tuple-element.10), channel_id=1, source_target_pairs={{12,0},{16,4},{20,8},{24,12},{28,16},{32,20},{36,24},{40,28},{44,3... | collective-permute-start | bytes 393224 | tf_op jit(solution)/shard_map/ppermute | solution.py:138
  41.2 2.8 %collective-permute-start.4 = (bf16[128,512]{1,0:T(8,128)(2,1)S(1)}, bf16[128,512]{1,0:T(8,128)(2,1)S(1)}, u32[]{:S(2)}, u32[]{:S(2)}) collective-permute-start(bf16[128,512]{1,0:T(8,128)(2,1)S(1)} %get-tuple-element.11), channel_id=1, source_target_pairs={{8,0},{12,4},{16,8},{20,12},{24,16},{28,20},{32,24},{36,28},{40,32... | collective-permute-start | bytes 393224 | tf_op jit(solution)/shard_map/ppermute | solution.py:138
  44.1 0.0 collective-permute-done.3
  44.1 1.9 %collective-permute-done.5 = bf16[128,512]{1,0:T(8,128)(2,1)S(1)} collective-permute-done((bf16[128,512]{1,0:T(8,128)(2,1)S(1)}, bf16[128,512]{1,0:T(8,128)(2,1)S(1)}, u32[]{:S(2)}, u32[]{:S(2)}) %collective-permute-start.5) | collective-permute-done | bytes 131104 | tf_op jit(solution)/shard_map/ppermute | solution.py:138
  46.0 2.8 %collective-permute-done.4 = bf16[128,512]{1,0:T(8,128)(2,1)S(1)} collective-permute-done((bf16[128,512]{1,0:T(8,128)(2,1)S(1)}, bf16[128,512]{1,0:T(8,128)(2,1)S(1)}, u32[]{:S(2)}, u32[]{:S(2)}) %collective-permute-start.4) | collective-permute-done | bytes 131104 | tf_op jit(solution)/shard_map/ppermute | solution.py:138
  48.8 0.1 add_convert_fusion
  48.9 15.1 %all_to_all.5 = bf16[4,32,512]{2,1,0:T(8,128)(2,1)S(1)} all-to-all(bf16[4,32,512]{2,1,0:T(8,128)(2,1)S(1)} %bitcast.16), channel_id=1, replica_groups=mesh['ctx'=128,'rec'=4] {'rec'}, dimensions={0} | all-to-all | bytes 262144 | tf_op jit(solution)/shard_map/all_to_all | solution.py:151
  64.0 0.6 fusion
  (3 shorter events, 0.1 us)
Async XLA Ops:
  0.6 0.9 %copy-start.1 = (bf16[128,256]{1,0:T(8,128)(2,1)S(1)}, bf16[128,256]{1,0:T(8,128)(2,1)}, u32[]{:S(2)}) copy-start(bf16[128,256]{1,0:T(8,128)(2,1)} %v_ref.1) | copy-start | bytes 196612
  1.5 21.5 %copy-start = (bf16[128,256]{1,0:T(8,128)(2,1)S(1)}, bf16[128,256]{1,0:T(8,128)(2,1)}, u32[]{:S(2)}) copy-start(bf16[128,256]{1,0:T(8,128)(2,1)} %k_ref.1) | copy-start | bytes 196612
  1.5 21.5 %copy-start.4 = (f32[1,32,128]{2,1,0:T(8,128)S(1)}, f32[1,32,128]{2,1,0:T(8,128)}, u32[]{:S(2)}) copy-start(f32[1,32,128]{2,1,0:T(8,128)} %param.9) | copy-start | bytes 49156
  1.5 21.5 %copy-start.5 = (f32[1,32,128]{2,1,0:T(8,128)S(1)}, f32[1,32,128]{2,1,0:T(8,128)}, u32[]{:S(2)}) copy-start(f32[1,32,128]{2,1,0:T(8,128)} %param.10) | copy-start | bytes 49156
  1.6 15.7 %collective-permute-start.2 = (bf16[128,512]{1,0:T(8,128)(2,1)S(1)}, bf16[128,512]{1,0:T(8,128)(2,1)S(1)}, u32[]{:S(2)}, u32[]{:S(2)}) collective-permute-start(bf16[128,512]{1,0:T(8,128)(2,1)S(1)} %constant_dynamic-update-slice_fusion), channel_id=1, source_target_pairs={{0,12},{4,16},{8,20},{12,24},{16,28},{20,32},{24,36},{28,40},{32,4... | collective-permute-start | bytes 393224 | tf_op jit(solution)/shard_map/ppermute | solution.py:138
  5.4 17.0 %collective-permute-start.1 = (bf16[128,512]{1,0:T(8,128)(2,1)S(1)}, bf16[128,512]{1,0:T(8,128)(2,1)S(1)}, u32[]{:S(2)}, u32[]{:S(2)}) collective-permute-start(bf16[128,512]{1,0:T(8,128)(2,1)S(1)} %constant_dynamic-update-slice_fusion), channel_id=1, source_target_pairs={{0,8},{4,12},{8,16},{12,20},{16,24},{20,28},{24,32},{28,36},{32,40... | collective-permute-start | bytes 393224 | tf_op jit(solution)/shard_map/ppermute | solution.py:138
  9.7 13.3 %collective-permute-start = (bf16[128,512]{1,0:T(8,128)(2,1)S(1)}, bf16[128,512]{1,0:T(8,128)(2,1)S(1)}, u32[]{:S(2)}, u32[]{:S(2)}) collective-permute-start(bf16[128,512]{1,0:T(8,128)(2,1)S(1)} %constant_dynamic-update-slice_fusion), channel_id=1, source_target_pairs={{0,4},{4,8},{8,12},{12,16},{16,20},{20,24},{24,28},{28,32},{32,36}... | collective-permute-start | bytes 393224 | tf_op jit(solution)/shard_map/ppermute | solution.py:138
  23.0 0.7 %copy-start.6 = (s32[1,128]{1,0:T(1,128)S(1)}, s32[1,128]{1,0:T(1,128)}, u32[]{:S(2)}) copy-start(s32[1,128]{1,0:T(1,128)} %ids.1) | copy-start | bytes 1540
  23.7 1.2 %copy-start.2 = (bf16[1,128,4096]{2,1,0:T(8,128)(2,1)S(1)}, bf16[1,128,4096]{2,1,0:T(8,128)(2,1)}, u32[]{:S(2)}) copy-start(bf16[1,128,4096]{2,1,0:T(8,128)(2,1)} %param.7) | copy-start | bytes 3145732
  24.9 1.2 %copy-start.3 = (bf16[1,128,4096]{2,1,0:T(8,128)(2,1)S(1)}, bf16[1,128,4096]{2,1,0:T(8,128)(2,1)}, u32[]{:S(2)}) copy-start(bf16[1,128,4096]{2,1,0:T(8,128)(2,1)} %param.8) | copy-start | bytes 3145732
  35.0 9.1 %collective-permute-start.3 = (bf16[128,512]{1,0:T(8,128)(2,1)S(1)}, bf16[128,512]{1,0:T(8,128)(2,1)S(1)}, u32[]{:S(2)}, u32[]{:S(2)}) collective-permute-start(bf16[128,512]{1,0:T(8,128)(2,1)S(1)} %get-tuple-element.9), channel_id=1, source_target_pairs={{4,0},{8,4},{12,8},{16,12},{20,16},{24,20},{28,24},{32,28},{36,32}... | collective-permute-start | bytes 393224 | tf_op jit(solution)/shard_map/ppermute | solution.py:138
  36.9 9.1 %collective-permute-start.5 = (bf16[128,512]{1,0:T(8,128)(2,1)S(1)}, bf16[128,512]{1,0:T(8,128)(2,1)S(1)}, u32[]{:S(2)}, u32[]{:S(2)}) collective-permute-start(bf16[128,512]{1,0:T(8,128)(2,1)S(1)} %get-tuple-element.10), channel_id=1, source_target_pairs={{12,0},{16,4},{20,8},{24,12},{28,16},{32,20},{36,24},{40,28},{44,3... | collective-permute-start | bytes 393224 | tf_op jit(solution)/shard_map/ppermute | solution.py:138
  41.2 7.6 %collective-permute-start.4 = (bf16[128,512]{1,0:T(8,128)(2,1)S(1)}, bf16[128,512]{1,0:T(8,128)(2,1)S(1)}, u32[]{:S(2)}, u32[]{:S(2)}) collective-permute-start(bf16[128,512]{1,0:T(8,128)(2,1)S(1)} %get-tuple-element.11), channel_id=1, source_target_pairs={{8,0},{12,4},{16,8},{20,12},{24,16},{28,20},{32,24},{36,28},{40,32... | collective-permute-start | bytes 393224 | tf_op jit(solution)/shard_map/ppermute | solution.py:138

commit v2 on v1

v2 whole, which is shorter than its diff:
```python
import functools
import math

import jax
import jax.numpy as jnp
from jax import lax
from jax.experimental import pallas as pl
from jax.experimental.pallas import tpu as pltpu
from jax.sharding import PartitionSpec as P

HD = 128
TOK = 128
SPAN = 4
HEADS = 32
GROUP = 16
CHUNK = 2
WIDTH = HEADS * HD
HALF = GROUP * HD
SCALE = HD**-0.5
LOG2E = math.log2(math.e)
FAR = 1e30
BF16 = jnp.bfloat16
F32 = jnp.float32
EARLY, LATE = (1, 2), (3,)

VMEM = pl.BlockSpec(memory_space=pltpu.VMEM)
HBM = pl.BlockSpec(memory_space=pltpu.HBM)
SMEM = pl.BlockSpec(memory_space=pltpu.SMEM)
SHAPE = jax.ShapeDtypeStruct
PART = SHAPE((TOK, 4 * HD), BF16)


def in_hbm(*arrays):
    return [pltpu.with_memory_space_constraint(a, pltpu.HBM) for a in arrays]


def in_vmem(*arrays):
    return [pltpu.with_memory_space_constraint(a, pltpu.VMEM) for a in arrays]


def settings(name, blocks, dots):
    return dict(
        name=name,
        compiler_params=pltpu.CompilerParams(vmem_limit_bytes=16 << 20),
        cost_estimate=pl.CostEstimate(
            flops=2 * dots * blocks * HEADS * TOK * TOK * HD,
            bytes_accessed=2 << 20,
            transcendentals=blocks * HEADS * TOK * TOK,
        ),
    )


def dot_nt(a, b):
    return lax.dot_general(a, b, (((1,), (1,)), ((), ())), preferred_element_type=F32)


def dot_nn(a, b):
    return lax.dot_general(a, b, (((1,), (0,)), ((), ())), preferred_element_type=F32)


def join_kernel(k, v, both, sem):
    copies = [
        pltpu.make_async_copy(k, both.at[:, : 2 * HD], sem.at[0]),
        pltpu.make_async_copy(v, both.at[:, 2 * HD :], sem.at[1]),
    ]
    for c in copies:
        c.start()
    for c in copies:
        c.wait()


def join(k, v):
    return pl.pallas_call(
        join_kernel,
        out_shape=PART,
        in_specs=[HBM, HBM],
        out_specs=VMEM,
        scratch_shapes=[pltpu.SemaphoreType.DMA((2,))],
        name="join",
    )(*in_hbm(k, v))


def head_rows(ref, head, count):
    return jnp.concatenate([ref[:, h * HD : (h + 1) * HD] for h in range(head, head + count)], 0)


def grad_tiles(g, both, away, causal, q_ref, o_ref, sums_ref, delta_ref, dscores, parts, probs):
    blocks = len(both)
    k = jnp.concatenate([b[:, g * HD : (g + 1) * HD] for b in both], 0)
    v = jnp.concatenate([b[:, (g + 2) * HD : (g + 3) * HD] for b in both], 0)

    def products(i):
        head = g * GROUP + i * CHUNK
        return dot_nt(k, head_rows(q_ref, head, CHUNK)), dot_nt(v, head_rows(o_ref, head, CHUNK))

    ahead = products(0)
    for i in range(GROUP // CHUNK):
        scores, dprobs = ahead
        if (i + 1) * CHUNK < GROUP:
            ahead = products(i + 1)
        p_cols, d_cols = [], []
        for j in range(CHUNK):
            head = g * GROUP + i * CHUNK + j
            sums = sums_ref[head : head + 1, :] * LOG2E
            delta = delta_ref[head : head + 1, :]
            p_rows, d_rows = [], []
            for b in range(blocks):
                tile = slice(b * TOK, (b + 1) * TOK), slice(j * TOK, (j + 1) * TOK)
                less = sums if away is None else sums + away[b]
                p = jnp.exp2(scores[tile] * (SCALE * LOG2E) - less)
                if causal is not None:
                    p = jnp.where(causal, p, 0.0)
                p_rows.append(p.astype(BF16))
                d_rows.append((p * (dprobs[tile] - delta)).astype(BF16))
            p_cols.append(jnp.concatenate(p_rows, 0))
            d_cols.append(jnp.concatenate(d_rows, 0))
        at = i * CHUNK * TOK
        probs[:, at : at + CHUNK * TOK] = jnp.concatenate(p_cols, 1)
        at += g * HALF
        dscores[:, at : at + CHUNK * TOK] = jnp.concatenate(d_cols, 1)
    value_grad = dot_nn(probs[...], head_rows(o_ref, g * GROUP, GROUP))
    key_grad = dot_nn(dscores[:, g * HALF : (g + 1) * HALF], head_rows(q_ref, g * GROUP, GROUP))
    for b, part in enumerate(parts):
        rows = slice(b * TOK, (b + 1) * TOK)
        part[:, g * HD : (g + 1) * HD] = (key_grad[rows] * SCALE).astype(part.dtype)
        part[:, (g + 2) * HD : (g + 3) * HD] = value_grad[rows].astype(part.dtype)


def distances(ids, blocks):
    me = lax.axis_index("ctx")
    away = []
    for back in blocks:
        at = jnp.maximum(me - back, 0)
        live = jnp.logical_and(me >= back, ids[0, at] == ids[0, me])
        away.append(jnp.where(live, F32(0.0), F32(FAR)))
    return away


def early_kernel(blocks, ids_hbm, q_hbm, o_hbm, sums_hbm, delta_hbm, *refs):
    n = len(blocks)
    both, refs = refs[:n], refs[n:]
    q, o, sums, delta, dscores = refs[:5]
    parts, (ids, probs, sem) = refs[5 : 5 + n], refs[5 + n :]
    small = [
        pltpu.make_async_copy(ids_hbm, ids, sem.at[0]),
        pltpu.make_async_copy(sums_hbm, sums, sem.at[1]),
        pltpu.make_async_copy(delta_hbm, delta, sem.at[2]),
    ]
    halves = []
    for g in range(2):
        cols = pl.ds(g * HALF, HALF)
        halves.append(
            [
                pltpu.make_async_copy(q_hbm.at[:, cols], q.at[:, cols], sem.at[3 + 2 * g]),
                pltpu.make_async_copy(o_hbm.at[:, cols], o.at[:, cols], sem.at[4 + 2 * g]),
            ]
        )
    for c in small + halves[0] + halves[1]:
        c.start()
    for c in small:
        c.wait()
    away = distances(ids, blocks)
    for g in range(2):
        for c in halves[g]:
            c.wait()
        grad_tiles(g, both, away, None, q, o, sums, delta, dscores, parts, probs)


def early(ids, q, o, sums, delta, both):
    n = len(both)
    return pl.pallas_call(
        functools.partial(early_kernel, EARLY),
        out_shape=[
            SHAPE(q.shape, BF16),
            SHAPE(o.shape, BF16),
            SHAPE(sums.shape, F32),
            SHAPE(delta.shape, F32),
            SHAPE((n * TOK, WIDTH), BF16),
        ]
        + [PART] * n,
        in_specs=[HBM] * 5 + [VMEM] * n,
        out_specs=[VMEM] * (5 + n),
        scratch_shapes=[
            pltpu.SMEM(ids.shape, jnp.int32),
            pltpu.VMEM((n * TOK, HALF), BF16),
            pltpu.SemaphoreType.DMA((7,)),
        ],
        **settings("early", n, 4),
    )(*in_hbm(ids, q, o, sums, delta), *both)


def late_kernel(blocks, ids, q, o, sums, delta, *refs):
    n = len(blocks)
    both, dscores, parts, probs = refs[:n], refs[n], refs[n + 1 : -1], refs[-1]
    away = distances(ids, blocks)
    for g in range(2):
        grad_tiles(g, both, away, None, q, o, sums, delta, dscores, parts, probs)


def late(ids, q, o, sums, delta, both):
    n = len(both)
    return pl.pallas_call(
        functools.partial(late_kernel, LATE),
        out_shape=[SHAPE((n * TOK, WIDTH), BF16)] + [PART] * n,
        in_specs=[SMEM] + [VMEM] * (4 + n),
        out_specs=[VMEM] * (1 + n),
        scratch_shapes=[pltpu.VMEM((n * TOK, HALF), BF16)],
        **settings("late", n, 4),
    )(ids, q, o, sums, delta, *both)


def own_kernel(q, o, sums, delta, *refs):
    both, dscores = refs[:SPAN], refs[SPAN : SPAN + 2]
    dq_hbm, part, dq, own, probs, sem = refs[SPAN + 2 :]
    key_at = lax.broadcasted_iota(jnp.int32, (TOK, TOK), 0)
    causal = key_at <= lax.broadcasted_iota(jnp.int32, (TOK, TOK), 1)
    copies = []
    for g in range(2):
        grad_tiles(g, both[:1], None, causal, q, o, sums, delta, own, (part,), probs)
        cols = slice(g * HALF, (g + 1) * HALF)
        kt = jnp.concatenate([b[:, g * HD : (g + 1) * HD].T for b in both], 1)
        d = jnp.concatenate([r[:, cols] for r in (own, *dscores)], 0)
        dqt = (dot_nn(kt, d) * SCALE).astype(BF16)
        for j in range(GROUP):
            at = g * HALF + j * HD
            dq[:, at : at + HD] = dqt[:, j * TOK : (j + 1) * TOK].T
        copies.append(pltpu.make_async_copy(dq.at[:, cols], dq_hbm.at[:, cols], sem.at[g]))
        copies[-1].start()
    for c in copies:
        c.wait()


def own(q, o, sums, delta, both, dscores):
    return pl.pallas_call(
        own_kernel,
        out_shape=[SHAPE(q.shape, BF16), SHAPE((TOK, 4 * HD), F32)],
        in_specs=[VMEM] * (4 + SPAN + 2),
        out_specs=[HBM, VMEM],
        scratch_shapes=[
            pltpu.VMEM((TOK, WIDTH), BF16),
            pltpu.VMEM((TOK, WIDTH), BF16),
            pltpu.VMEM((TOK, HALF), BF16),
            pltpu.SemaphoreType.DMA((2,)),
        ],
        **settings("own", 2, 4),
    )(*in_vmem(q, o, sums, delta, *both, *dscores))


def shifted(block, by):
    devices = range(lax.axis_size("ctx"))
    return lax.ppermute(block, "ctx", [(i, i + by) for i in devices if i + by in devices])


def per_device(queries, out_grads, log_sums, deltas, keys, values, doc_ids):
    both = [join(keys, values)]
    both += [shifted(both[0], by) for by in range(1, SPAN)]
    q, o, sums, delta, far, *parts = early(
        doc_ids, queries[0], out_grads[0], log_sums[0], deltas[0], [both[b] for b in EARLY]
    )
    farther, *others = late(doc_ids, q, o, sums, delta, [both[b] for b in LATE])
    parts += others
    query_grad, total = own(q, o, sums, delta, both, (far, farther))
    for by in range(1, SPAN):
        total = total + shifted(parts[by - 1], -by).astype(F32)
    peers = lax.axis_size("rec")
    pieces = total.astype(BF16).reshape(peers, TOK // peers, -1)
    arrived = lax.all_to_all(pieces, "rec", 0, 0, tiled=True)
    summed = arrived.astype(F32).sum(axis=0).astype(BF16)
    return query_grad[None], summed[:, : 2 * HD], summed[:, 2 * HD :]


def solution(mesh):
    return jax.shard_map(
        per_device,
        mesh=mesh,
        in_specs=(
            P("rec", "ctx", None),
            P("rec", "ctx", None),
            P("rec", None, "ctx"),
            P("rec", None, "ctx"),
            P("ctx", None),
            P("ctx", None),
            P("rec", None),
        ),
        out_specs=(P("rec", "ctx", None), P(("ctx", "rec"), None), P(("ctx", "rec"), None)),
        check_vma=False,
    )
```

time: 65 us -> 55.5 us (0.85)
  the two profiles are of different devices: /device:TPU:6 before, /device:TPU:7 now
where the time goes in v2:
time: 55.5 us; the launch traced here: 55.2 us
  starting transfers between devices  24.1 us (43%)
  blocking collectives  14.6 us (26%)
  Pallas kernels  10.2 us (18%)
  waiting for transfers between devices  4.84 us (9%)
  between operations  0.77 us (1%)
  local copies, waits for them, and re-layouts  0.63 us (1%)
    ppermute x6, starting transfers between devices, shifted(): lax.ppermute(block, 'ctx', [(i, i + by) for i in devices if i + by in dev...  24.1 us
    all_to_all x1, blocking collectives, per_device(): arrived = lax.all_to_all(pieces, 'rec', 0, 0, tiled=True)  14.6 us
    ppermute x6, waiting for transfers between devices, shifted(): lax.ppermute(block, 'ctx', [(i, i + by) for i in devices if i + by in dev...  4.84 us
    pallas_call x1, Pallas kernels, early(): pl.pallas_call(functools.partial(early_kernel, EARLY), out_shape=[SHAPE(q...  3.84 us
    pallas_call x1, Pallas kernels, own(): pl.pallas_call(own_kernel, out_shape=[SHAPE(q.shape, BF16), SHAPE((TOK, 4...  2.95 us
    pallas_call x1, Pallas kernels, late(): pl.pallas_call(functools.partial(late_kernel, LATE), out_shape=[SHAPE((n...  1.84 us
    pallas_call x1, Pallas kernels, join(): pl.pallas_call(join_kernel, out_shape=PART, in_specs=[HBM, HBM], out_spec...  1.55 us
  transfers between devices with their start and end apart: 6, of which 2 were waited for; matrix products, arithmetic and copies ran while one was open for 0% of the time, Pallas kernels for 16%

profile of v2, /device:TPU:7, one launch (start us, length us, event | category | flops | bytes accessed | tf_op | source)
XLA Modules:
  0.0 55.2 jit_solution(1171769139270410000)
XLA Ops:
  0.6 0.0 copy-start.1
  0.6 1.5 %join.1.refs_0_ = bf16[128,512]{1,0:T(8,128)(2,1)} custom-call(bf16[128,256]{1,0:T(8,128)(2,1)} %k.1, bf16[128,256]{1,0:T(8,128)(2,1)} %v.1), custom_call_target="tpu_custom_call" | custom-call | tf_op jit(solution)/shard_map/join/pallas_call | solution.py:73
  2.2 4.0 %collective-permute-start.1 = (bf16[128,512]{1,0:T(8,128)(2,1)}, bf16[128,512]{1,0:T(8,128)(2,1)S(1)}, u32[]{:S(2)}, u32[]{:S(2)}) collective-permute-start(bf16[128,512]{1,0:T(8,128)(2,1)} %join.1.refs_0_), channel_id=1, source_target_pairs={{0,8},{4,12},{8,16},{12,20},{16,24},{20,28},{24,32},{28,36},{32,40... | collective-permute-start | bytes 393224 | tf_op jit(solution)/shard_map/ppermute | solution.py:251
  6.2 4.8 %collective-permute-start = (bf16[128,512]{1,0:T(8,128)(2,1)}, bf16[128,512]{1,0:T(8,128)(2,1)S(1)}, u32[]{:S(2)}, u32[]{:S(2)}) collective-permute-start(bf16[128,512]{1,0:T(8,128)(2,1)} %join.1.refs_0_), channel_id=1, source_target_pairs={{0,4},{4,8},{8,12},{12,16},{16,20},{20,24},{24,28},{28,32},{32,36}... | collective-permute-start | bytes 393224 | tf_op jit(solution)/shard_map/ppermute | solution.py:251
  11.1 3.7 %collective-permute-start.2 = (bf16[128,512]{1,0:T(8,128)(2,1)}, bf16[128,512]{1,0:T(8,128)(2,1)S(1)}, u32[]{:S(2)}, u32[]{:S(2)}) collective-permute-start(bf16[128,512]{1,0:T(8,128)(2,1)} %join.1.refs_0_), channel_id=1, source_target_pairs={{0,12},{4,16},{8,20},{12,24},{16,28},{20,32},{24,36},{28,40},{32,4... | collective-permute-start | bytes 393224 | tf_op jit(solution)/shard_map/ppermute | solution.py:251
  14.8 2.8 %collective-permute-done.1.refs_1_.refs_2_ = bf16[128,512]{1,0:T(8,128)(2,1)S(1)} collective-permute-done((bf16[128,512]{1,0:T(8,128)(2,1)}, bf16[128,512]{1,0:T(8,128)(2,1)S(1)}, u32[]{:S(2)}, u32[]{:S(2)}) %collective-permute-start.1) | collective-permute-done | bytes 131104 | tf_op jit(solution)/shard_map/ppermute | solution.py:251
  17.6 0.0 collective-permute-done.refs_0_.refs_1_
  17.6 3.8 %early.1 = (bf16[128,4096]{1,0:T(8,128)(2,1)S(1)}, bf16[128,4096]{1,0:T(8,128)(2,1)S(1)}, f32[32,128]{1,0:T(8,128)S(1)}, f32[32,128]{1,0:T(8,128)S(1)}, bf16[256...) custom-call(s32[1,128]{1,0:T(1,128)} %ids.1, bf16[128,4096]{1,0:T(8,128)(2,1)} %bitcast.7, ...), custom_call_target="tpu_custom_call" | custom-call | flops 1073741824 | bytes 2097152 | tf_op jit(solution)/shard_map/early/pallas_call | solution.py:171
  21.4 0.0 copy-start
  21.4 4.7 %collective-permute-start.3 = (bf16[128,512]{1,0:T(8,128)(2,1)S(1)}, bf16[128,512]{1,0:T(8,128)(2,1)S(1)}, u32[]{:S(2)}, u32[]{:S(2)}) collective-permute-start(bf16[128,512]{1,0:T(8,128)(2,1)S(1)} %get-tuple-element.22), channel_id=1, source_target_pairs={{4,0},{8,4},{12,8},{16,12},{20,16},{24,20},{28,24},{32,28},{36,32}... | collective-permute-start | bytes 393224 | tf_op jit(solution)/shard_map/ppermute | solution.py:251
  26.1 3.4 %collective-permute-start.4 = (bf16[128,512]{1,0:T(8,128)(2,1)S(1)}, bf16[128,512]{1,0:T(8,128)(2,1)S(1)}, u32[]{:S(2)}, u32[]{:S(2)}) collective-permute-start(bf16[128,512]{1,0:T(8,128)(2,1)S(1)} %get-tuple-element.23), channel_id=1, source_target_pairs={{8,0},{12,4},{16,8},{20,12},{24,16},{28,20},{32,24},{36,28},{40,32... | collective-permute-start | bytes 393224 | tf_op jit(solution)/shard_map/ppermute | solution.py:251
  29.5 0.0 collective-permute-done.2.refs_0_.refs_3_
  29.5 0.0 copy-done.1
  29.5 1.8 %late.1 = (bf16[128,4096]{1,0:T(8,128)(2,1)S(1)}, bf16[128,512]{1,0:T(8,128)(2,1)S(1)}) custom-call(s32[1,128]{1,0:T(1,128)S(1)} %copy-done.1, bf16[128,4096]{1,0:T(8,128)(2,1)S(1)} %get-tuple-element.14.q, bf16[128,4096]{1,0:T(8,128)(2,1)S(1)} %get-tuple-element.15.o, f32[32,128]{1,0:T(8,128)S(1)} %get-tuple-element.16.sums, ...), custom_call_target="tpu_custom_call" | custom-call | flops 536870912 | bytes 2097152 | tf_op jit(solution)/shard_map/late/pallas_call | solution.py:202
  31.3 3.5 %collective-permute-start.5 = (bf16[128,512]{1,0:T(8,128)(2,1)S(1)}, bf16[128,512]{1,0:T(8,128)(2,1)S(1)}, u32[]{:S(2)}, u32[]{:S(2)}) collective-permute-start(bf16[128,512]{1,0:T(8,128)(2,1)S(1)} %get-tuple-element.24), channel_id=1, source_target_pairs={{12,0},{16,4},{20,8},{24,12},{28,16},{32,20},{36,24},{40,28},{44,3... | collective-permute-start | bytes 393224 | tf_op jit(solution)/shard_map/ppermute | solution.py:251
  34.9 0.0 copy-done
  34.9 2.9 %own.1 = (bf16[128,4096]{1,0:T(8,128)(2,1)}, f32[128,512]{1,0:T(8,128)S(1)}) custom-call(bf16[128,4096]{1,0:T(8,128)(2,1)S(1)} %get-tuple-element.14.q, bf16[128,4096]{1,0:T(8,128)(2,1)S(1)} %get-tuple-element.15.o, f32[32,128]{1,0:T(8,128)S(1)} %get-tuple-element.16.sums, f32[32,128]{1,0:T(8,128)S(1)} %get-tuple-element.17.delta, ...), custom_call_target="tpu_custom_call" | custom-call | flops 1073741824 | bytes 2097152 | tf_op jit(solution)/shard_map/own/pallas_call | solution.py:234
  37.8 0.0 collective-permute-done.3
  37.8 0.0 collective-permute-done.4
  37.8 2.1 %collective-permute-done.5 = bf16[128,512]{1,0:T(8,128)(2,1)S(1)} collective-permute-done((bf16[128,512]{1,0:T(8,128)(2,1)S(1)}, bf16[128,512]{1,0:T(8,128)(2,1)S(1)}, u32[]{:S(2)}, u32[]{:S(2)}) %collective-permute-start.5) | collective-permute-done | bytes 131104 | tf_op jit(solution)/shard_map/ppermute | solution.py:251
  39.9 0.1 add_convert_fusion
  40.0 14.6 %all_to_all.5 = bf16[4,32,512]{2,1,0:T(8,128)(2,1)S(1)} all-to-all(bf16[4,32,512]{2,1,0:T(8,128)(2,1)S(1)} %bitcast.6), channel_id=1, replica_groups=mesh['ctx'=128,'rec'=4] {'rec'}, dimensions={0} | all-to-all | bytes 262144 | tf_op jit(solution)/shard_map/all_to_all | solution.py:267
  54.5 0.6 %fusion = (bf16[32,256]{1,0:T(8,128)(2,1)}, bf16[32,256]{1,0:T(8,128)(2,1)}) fusion(bf16[32,512]{1,0:T(8,128)(2,1)S(1)} %reduce_sum.12), kind=kLoop, calls=%fused_computation.1 | loop fusion | bytes 65536 | tf_op jit(solution)/shard_map/slice | solution.py:269
  (1 shorter events, 0.0 us)
Async XLA Ops:
  0.6 28.9 %copy-start.1 = (s32[1,128]{1,0:T(1,128)S(1)}, s32[1,128]{1,0:T(1,128)}, u32[]{:S(2)}) copy-start(s32[1,128]{1,0:T(1,128)} %ids.1) | copy-start | bytes 1540
  2.2 15.4 %collective-permute-start.1 = (bf16[128,512]{1,0:T(8,128)(2,1)}, bf16[128,512]{1,0:T(8,128)(2,1)S(1)}, u32[]{:S(2)}, u32[]{:S(2)}) collective-permute-start(bf16[128,512]{1,0:T(8,128)(2,1)} %join.1.refs_0_), channel_id=1, source_target_pairs={{0,8},{4,12},{8,16},{12,20},{16,24},{20,28},{24,32},{28,36},{32,40... | collective-permute-start | bytes 393224 | tf_op jit(solution)/shard_map/ppermute | solution.py:251
  6.2 11.4 %collective-permute-start = (bf16[128,512]{1,0:T(8,128)(2,1)}, bf16[128,512]{1,0:T(8,128)(2,1)S(1)}, u32[]{:S(2)}, u32[]{:S(2)}) collective-permute-start(bf16[128,512]{1,0:T(8,128)(2,1)} %join.1.refs_0_), channel_id=1, source_target_pairs={{0,4},{4,8},{8,12},{12,16},{16,20},{20,24},{24,28},{28,32},{32,36}... | collective-permute-start | bytes 393224 | tf_op jit(solution)/shard_map/ppermute | solution.py:251
  11.1 18.4 %collective-permute-start.2 = (bf16[128,512]{1,0:T(8,128)(2,1)}, bf16[128,512]{1,0:T(8,128)(2,1)S(1)}, u32[]{:S(2)}, u32[]{:S(2)}) collective-permute-start(bf16[128,512]{1,0:T(8,128)(2,1)} %join.1.refs_0_), channel_id=1, source_target_pairs={{0,12},{4,16},{8,20},{12,24},{16,28},{20,32},{24,36},{28,40},{32,4... | collective-permute-start | bytes 393224 | tf_op jit(solution)/shard_map/ppermute | solution.py:251
  21.4 13.4 %copy-start = (bf16[128,512]{1,0:T(8,128)(2,1)S(1)}, bf16[128,512]{1,0:T(8,128)(2,1)}, u32[]{:S(2)}) copy-start(bf16[128,512]{1,0:T(8,128)(2,1)} %join.1.refs_0_) | copy-start | bytes 393220
  21.4 16.4 %collective-permute-start.3 = (bf16[128,512]{1,0:T(8,128)(2,1)S(1)}, bf16[128,512]{1,0:T(8,128)(2,1)S(1)}, u32[]{:S(2)}, u32[]{:S(2)}) collective-permute-start(bf16[128,512]{1,0:T(8,128)(2,1)S(1)} %get-tuple-element.22), channel_id=1, source_target_pairs={{4,0},{8,4},{12,8},{16,12},{20,16},{24,20},{28,24},{32,28},{36,32}... | collective-permute-start | bytes 393224 | tf_op jit(solution)/shard_map/ppermute | solution.py:251
  26.1 11.7 %collective-permute-start.4 = (bf16[128,512]{1,0:T(8,128)(2,1)S(1)}, bf16[128,512]{1,0:T(8,128)(2,1)S(1)}, u32[]{:S(2)}, u32[]{:S(2)}) collective-permute-start(bf16[128,512]{1,0:T(8,128)(2,1)S(1)} %get-tuple-element.23), channel_id=1, source_target_pairs={{8,0},{12,4},{16,8},{20,12},{24,16},{28,20},{32,24},{36,28},{40,32... | collective-permute-start | bytes 393224 | tf_op jit(solution)/shard_map/ppermute | solution.py:251
  31.3 8.5 %collective-permute-start.5 = (bf16[128,512]{1,0:T(8,128)(2,1)S(1)}, bf16[128,512]{1,0:T(8,128)(2,1)S(1)}, u32[]{:S(2)}, u32[]{:S(2)}) collective-permute-start(bf16[128,512]{1,0:T(8,128)(2,1)S(1)} %get-tuple-element.24), channel_id=1, source_target_pairs={{12,0},{16,4},{20,8},{24,12},{28,16},{32,20},{36,24},{40,28},{44,3... | collective-permute-start | bytes 393224 | tf_op jit(solution)/shard_map/ppermute | solution.py:251

commit v3 on v2

--- a/solution.py
+++ b/solution.py
@@ -21,7 +21,7 @@
 FAR = 1e30
 BF16 = jnp.bfloat16
 F32 = jnp.float32
-EARLY, LATE = (1, 2), (3,)
+EARLY, LATE = (3,), (2, 1)
 
 VMEM = pl.BlockSpec(memory_space=pltpu.VMEM)
 HBM = pl.BlockSpec(memory_space=pltpu.HBM)
@@ -38,10 +38,10 @@
     return [pltpu.with_memory_space_constraint(a, pltpu.VMEM) for a in arrays]
 
 
-def settings(name, blocks, dots):
+def settings(name, blocks, dots, mib):
     return dict(
         name=name,
-        compiler_params=pltpu.CompilerParams(vmem_limit_bytes=16 << 20),
+        compiler_params=pltpu.CompilerParams(vmem_limit_bytes=mib << 20),
         cost_estimate=pl.CostEstimate(
             flops=2 * dots * blocks * HEADS * TOK * TOK * HD,
             bytes_accessed=2 << 20,
@@ -76,7 +76,7 @@
         in_specs=[HBM, HBM],
         out_specs=VMEM,
         scratch_shapes=[pltpu.SemaphoreType.DMA((2,))],
-        name="join",
+        **settings("join", 0, 0, 1),
     )(*in_hbm(k, v))
 
 
@@ -136,60 +136,28 @@
     return away
 
 
-def early_kernel(blocks, ids_hbm, q_hbm, o_hbm, sums_hbm, delta_hbm, *refs):
-    n = len(blocks)
-    both, refs = refs[:n], refs[n:]
-    q, o, sums, delta, dscores = refs[:5]
-    parts, (ids, probs, sem) = refs[5 : 5 + n], refs[5 + n :]
-    small = [
-        pltpu.make_async_copy(ids_hbm, ids, sem.at[0]),
-        pltpu.make_async_copy(sums_hbm, sums, sem.at[1]),
-        pltpu.make_async_copy(delta_hbm, delta, sem.at[2]),
-    ]
-    halves = []
-    for g in range(2):
-        cols = pl.ds(g * HALF, HALF)
-        halves.append(
-            [
-                pltpu.make_async_copy(q_hbm.at[:, cols], q.at[:, cols], sem.at[3 + 2 * g]),
-                pltpu.make_async_copy(o_hbm.at[:, cols], o.at[:, cols], sem.at[4 + 2 * g]),
-            ]
-        )
-    for c in small + halves[0] + halves[1]:
+def load_kernel(*refs):
+    n = len(refs) // 2
+    copies = [pltpu.make_async_copy(refs[i], refs[n + i], refs[-1].at[i]) for i in range(n)]
+    for c in copies:
         c.start()
-    for c in small:
+    for c in copies:
         c.wait()
-    away = distances(ids, blocks)
-    for g in range(2):
-        for c in halves[g]:
-            c.wait()
-        grad_tiles(g, both, away, None, q, o, sums, delta, dscores, parts, probs)
-
-
-def early(ids, q, o, sums, delta, both):
-    n = len(both)
-    return pl.pallas_call(
-        functools.partial(early_kernel, EARLY),
-        out_shape=[
-            SHAPE(q.shape, BF16),
-            SHAPE(o.shape, BF16),
-            SHAPE(sums.shape, F32),
-            SHAPE(delta.shape, F32),
-            SHAPE((n * TOK, WIDTH), BF16),
-        ]
-        + [PART] * n,
-        in_specs=[HBM] * 5 + [VMEM] * n,
-        out_specs=[VMEM] * (5 + n),
-        scratch_shapes=[
-            pltpu.SMEM(ids.shape, jnp.int32),
-            pltpu.VMEM((n * TOK, HALF), BF16),
-            pltpu.SemaphoreType.DMA((7,)),
-        ],
-        **settings("early", n, 4),
-    )(*in_hbm(ids, q, o, sums, delta), *both)
-
-
-def late_kernel(blocks, ids, q, o, sums, delta, *refs):
+
+
+def load(*arrays):
+    n = len(arrays)
+    return pl.pallas_call(
+        load_kernel,
+        out_shape=[SHAPE(a.shape, a.dtype) for a in arrays],
+        in_specs=[HBM] * n,
+        out_specs=[VMEM] * n,
+        scratch_shapes=[pltpu.SemaphoreType.DMA((n,))],
+        **settings("load", 1, 1, 2),
+    )(*in_hbm(*arrays))
+
+
+def behind_kernel(blocks, ids, q, o, sums, delta, *refs):
     n = len(blocks)
     both, dscores, parts, probs = refs[:n], refs[n], refs[n + 1 : -1], refs[-1]
     away = distances(ids, blocks)
@@ -197,16 +165,16 @@
         grad_tiles(g, both, away, None, q, o, sums, delta, dscores, parts, probs)
 
 
-def late(ids, q, o, sums, delta, both):
-    n = len(both)
-    return pl.pallas_call(
-        functools.partial(late_kernel, LATE),
+def behind(name, blocks, ids, q, o, sums, delta, both):
+    n = len(blocks)
+    return pl.pallas_call(
+        functools.partial(behind_kernel, blocks),
         out_shape=[SHAPE((n * TOK, WIDTH), BF16)] + [PART] * n,
         in_specs=[SMEM] + [VMEM] * (4 + n),
         out_specs=[VMEM] * (1 + n),
         scratch_shapes=[pltpu.VMEM((n * TOK, HALF), BF16)],
-        **settings("late", n, 4),
-    )(ids, q, o, sums, delta, *both)
+        **settings(name, n, 4, 12),
+    )(ids, q, o, sums, delta, *[both[b] for b in blocks])
 
 
 def own_kernel(q, o, sums, delta, *refs):
@@ -242,7 +210,7 @@
             pltpu.VMEM((TOK, HALF), BF16),
             pltpu.SemaphoreType.DMA((2,)),
         ],
-        **settings("own", 2, 4),
+        **settings("own", 2, 4, 12),
     )(*in_vmem(q, o, sums, delta, *both, *dscores))
 
 
@@ -254,14 +222,14 @@
 def per_device(queries, out_grads, log_sums, deltas, keys, values, doc_ids):
     both = [join(keys, values)]
     both += [shifted(both[0], by) for by in range(1, SPAN)]
-    q, o, sums, delta, far, *parts = early(
-        doc_ids, queries[0], out_grads[0], log_sums[0], deltas[0], [both[b] for b in EARLY]
-    )
-    farther, *others = late(doc_ids, q, o, sums, delta, [both[b] for b in LATE])
-    parts += others
-    query_grad, total = own(q, o, sums, delta, both, (far, farther))
+    q, o, sums, delta = load(queries[0], out_grads[0], log_sums[0], deltas[0])
+    far, *parts = behind("early", EARLY, doc_ids, q, o, sums, delta, both)
+    farther, *others = behind("late", LATE, doc_ids, q, o, sums, delta, both)
+    parts = dict(zip(EARLY + LATE, parts + others))
+    ordered = [both[b] for b in (0, *EARLY, *LATE)]
+    query_grad, total = own(q, o, sums, delta, ordered, (far, farther))
     for by in range(1, SPAN):
-        total = total + shifted(parts[by - 1], -by).astype(F32)
+        total = total + shifted(parts[by], -by).astype(F32)
     peers = lax.axis_size("rec")
     pieces = total.astype(BF16).reshape(peers, TOK // peers, -1)
     arrived = lax.all_to_all(pieces, "rec", 0, 0, tiled=True)

time: 55.5 us -> 53 us (0.955)
  the two profiles are of different devices: /device:TPU:7 before, /device:TPU:6 now
where the time goes in v3:
time: 53 us; the launch traced here: 52.7 us
  starting transfers between devices  24.1 us (45%)
  blocking collectives  14.8 us (28%)
  Pallas kernels  10.2 us (19%)
  waiting for transfers between devices  2.15 us (4%)
  between operations  0.76 us (1%)
  local copies, waits for them, and re-layouts  0.62 us (1%)
    ppermute x6, starting transfers between devices, shifted(): lax.ppermute(block, 'ctx', [(i, i + by) for i in devices if i + by in dev...  24.1 us
    all_to_all x1, blocking collectives, per_device(): arrived = lax.all_to_all(pieces, 'rec', 0, 0, tiled=True)  14.8 us
    pallas_call x2, Pallas kernels, behind(): pl.pallas_call(functools.partial(behind_kernel, blocks), out_shape=[SHAPE...  4.75 us
    pallas_call x1, Pallas kernels, own(): pl.pallas_call(own_kernel, out_shape=[SHAPE(q.shape, BF16), SHAPE((TOK, 4...  2.96 us
    ppermute x6, waiting for transfers between devices, shifted(): lax.ppermute(block, 'ctx', [(i, i + by) for i in devices if i + by in dev...  2.15 us
    pallas_call x1, Pallas kernels, load(): pl.pallas_call(load_kernel, out_shape=[SHAPE(a.shape, a.dtype) for a in a...  1.58 us
  transfers between devices with their start and end apart: 6, of which 2 were waited for; matrix products, arithmetic and copies ran while one was open for 0% of the time, Pallas kernels for 18%

profile of v3, /device:TPU:6, one launch (start us, length us, event | category | flops | bytes accessed | tf_op | source)
XLA Modules:
  0.0 52.7 jit_solution(7756838093717161385)
XLA Ops:
  0.6 0.0 copy-start
  0.6 0.9 %join.1.refs_0_ = bf16[128,512]{1,0:T(8,128)(2,1)S(1)} custom-call(bf16[128,256]{1,0:T(8,128)(2,1)} %k.1, bf16[128,256]{1,0:T(8,128)(2,1)} %v.1), custom_call_target="tpu_custom_call" | custom-call | bytes 2097152 | tf_op jit(solution)/shard_map/join/pallas_call | solution.py:73
  1.5 3.7 %collective-permute-start = (bf16[128,512]{1,0:T(8,128)(2,1)S(1)}, bf16[128,512]{1,0:T(8,128)(2,1)S(1)}, u32[]{:S(2)}, u32[]{:S(2)}) collective-permute-start(bf16[128,512]{1,0:T(8,128)(2,1)S(1)} %join.1.refs_0_), channel_id=1, source_target_pairs={{0,12},{4,16},{8,20},{12,24},{16,28},{20,32},{24,36},{28,40},{32,4... | collective-permute-start | bytes 393224 | tf_op jit(solution)/shard_map/ppermute | solution.py:219
  5.3 4.4 %collective-permute-start.2 = (bf16[128,512]{1,0:T(8,128)(2,1)S(1)}, bf16[128,512]{1,0:T(8,128)(2,1)S(1)}, u32[]{:S(2)}, u32[]{:S(2)}) collective-permute-start(bf16[128,512]{1,0:T(8,128)(2,1)S(1)} %join.1.refs_0_), channel_id=1, source_target_pairs={{0,4},{4,8},{8,12},{12,16},{16,20},{20,24},{24,28},{28,32},{32,36}... | collective-permute-start | bytes 393224 | tf_op jit(solution)/shard_map/ppermute | solution.py:219
  9.7 4.3 %collective-permute-start.1 = (bf16[128,512]{1,0:T(8,128)(2,1)S(1)}, bf16[128,512]{1,0:T(8,128)(2,1)S(1)}, u32[]{:S(2)}, u32[]{:S(2)}) collective-permute-start(bf16[128,512]{1,0:T(8,128)(2,1)S(1)} %join.1.refs_0_), channel_id=1, source_target_pairs={{0,8},{4,12},{8,16},{12,20},{16,24},{20,28},{24,32},{28,36},{32,40... | collective-permute-start | bytes 393224 | tf_op jit(solution)/shard_map/ppermute | solution.py:219
  14.0 1.6 %load.1 = (bf16[128,4096]{1,0:T(8,128)(2,1)S(1)}, bf16[128,4096]{1,0:T(8,128)(2,1)S(1)}, f32[32,128]{1,0:T(8,128)S(1)}, f32[32,128]{1,0:T(8,128)S(1)}) custom-call(bf16[128,4096]{1,0:T(8,128)(2,1)} %bitcast.6, bf16[128,4096]{1,0:T(8,128)(2,1)} %bitcast.7, f32[32,128]{1,0:T(8,128)} %bitcast.9, f32[32,128]{1,0:T(8,128)} %bitcast.10), custom_call_target="tpu_custom_call" | custom-call | flops 134217728 | bytes 2097152 | tf_op jit(solution)/shard_map/load/pallas_call | solution.py:150
  15.6 1.6 %collective-permute-done.refs_0_.refs_1_ = bf16[128,512]{1,0:T(8,128)(2,1)S(1)} collective-permute-done((bf16[128,512]{1,0:T(8,128)(2,1)S(1)}, bf16[128,512]{1,0:T(8,128)(2,1)S(1)}, u32[]{:S(2)}, u32[]{:S(2)}) %collective-permute-start) | collective-permute-done | bytes 131104 | tf_op jit(solution)/shard_map/ppermute | solution.py:219
  17.1 0.0 copy-done
  17.1 1.8 %early.1 = (bf16[128,4096]{1,0:T(8,128)(2,1)S(1)}, bf16[128,512]{1,0:T(8,128)(2,1)S(1)}) custom-call(s32[1,128]{1,0:T(1,128)S(1)} %copy-done, bf16[128,4096]{1,0:T(8,128)(2,1)S(1)} %get-tuple-element.14.q, bf16[128,4096]{1,0:T(8,128)(2,1)S(1)} %get-tuple-element.15.o, f32[32,128]{1,0:T(8,128)S(1)} %get-tuple-element.16.sums, ...), custom_call_target="tpu_custom_call" | custom-call | flops 536870912 | bytes 2097152 | tf_op jit(solution)/shard_map/early/pallas_call | solution.py:170
  19.0 5.2 %collective-permute-start.5 = (bf16[128,512]{1,0:T(8,128)(2,1)S(1)}, bf16[128,512]{1,0:T(8,128)(2,1)S(1)}, u32[]{:S(2)}, u32[]{:S(2)}) collective-permute-start(bf16[128,512]{1,0:T(8,128)(2,1)S(1)} %get-tuple-element.24), channel_id=1, source_target_pairs={{12,0},{16,4},{20,8},{24,12},{28,16},{32,20},{36,24},{40,28},{44,3... | collective-permute-start | bytes 393224 | tf_op jit(solution)/shard_map/ppermute | solution.py:219
  24.2 0.0 collective-permute-done.2.refs_1_.refs_3_
  24.2 0.0 collective-permute-done.1.refs_0_.refs_2_
  24.2 2.9 %late.1 = (bf16[256,4096]{1,0:T(8,128)(2,1)S(1)}, bf16[128,512]{1,0:T(8,128)(2,1)S(1)}, bf16[128,512]{1,0:T(8,128)(2,1)S(1)}) custom-call(s32[1,128]{1,0:T(1,128)S(1)} %copy-done, bf16[128,4096]{1,0:T(8,128)(2,1)S(1)} %get-tuple-element.14.q, bf16[128,4096]{1,0:T(8,128)(2,1)S(1)} %get-tuple-element.15.o, f32[32,128]{1,0:T(8,128)S(1)} %get-tuple-element.16.sums, ...), custom_call_target="tpu_custom_call" | custom-call | flops 1073741824 | bytes 2097152 | tf_op jit(solution)/shard_map/late/pallas_call | solution.py:170
  27.1 2.5 %collective-permute-start.3 = (bf16[128,512]{1,0:T(8,128)(2,1)S(1)}, bf16[128,512]{1,0:T(8,128)(2,1)S(1)}, u32[]{:S(2)}, u32[]{:S(2)}) collective-permute-start(bf16[128,512]{1,0:T(8,128)(2,1)S(1)} %get-tuple-element.22), channel_id=1, source_target_pairs={{4,0},{8,4},{12,8},{16,12},{20,16},{24,20},{28,24},{32,28},{36,32}... | collective-permute-start | bytes 393224 | tf_op jit(solution)/shard_map/ppermute | solution.py:219
  29.6 4.0 %collective-permute-start.4 = (bf16[128,512]{1,0:T(8,128)(2,1)S(1)}, bf16[128,512]{1,0:T(8,128)(2,1)S(1)}, u32[]{:S(2)}, u32[]{:S(2)}) collective-permute-start(bf16[128,512]{1,0:T(8,128)(2,1)S(1)} %get-tuple-element.23), channel_id=1, source_target_pairs={{8,0},{12,4},{16,8},{20,12},{24,16},{28,20},{32,24},{36,28},{40,32... | collective-permute-start | bytes 393224 | tf_op jit(solution)/shard_map/ppermute | solution.py:219
  33.6 3.0 %own.1 = (bf16[128,4096]{1,0:T(8,128)(2,1)}, f32[128,512]{1,0:T(8,128)S(1)}) custom-call(bf16[128,4096]{1,0:T(8,128)(2,1)S(1)} %get-tuple-element.14.q, bf16[128,4096]{1,0:T(8,128)(2,1)S(1)} %get-tuple-element.15.o, f32[32,128]{1,0:T(8,128)S(1)} %get-tuple-element.16.sums, f32[32,128]{1,0:T(8,128)S(1)} %get-tuple-element.17.delta, ...), custom_call_target="tpu_custom_call" | custom-call | flops 1073741824 | bytes 2097152 | tf_op jit(solution)/shard_map/own/pallas_call | solution.py:202
  36.6 0.0 collective-permute-done.5
  36.6 0.0 collective-permute-done.3
  36.6 0.5 %collective-permute-done.4 = bf16[128,512]{1,0:T(8,128)(2,1)S(1)} collective-permute-done((bf16[128,512]{1,0:T(8,128)(2,1)S(1)}, bf16[128,512]{1,0:T(8,128)(2,1)S(1)}, u32[]{:S(2)}, u32[]{:S(2)}) %collective-permute-start.4) | collective-permute-done | bytes 131104 | tf_op jit(solution)/shard_map/ppermute | solution.py:219
  37.2 0.1 add_convert_fusion
  37.2 14.8 %all_to_all.5 = bf16[4,32,512]{2,1,0:T(8,128)(2,1)S(1)} all-to-all(bf16[4,32,512]{2,1,0:T(8,128)(2,1)S(1)} %bitcast.8), channel_id=1, replica_groups=mesh['ctx'=128,'rec'=4] {'rec'}, dimensions={0} | all-to-all | bytes 262144 | tf_op jit(solution)/shard_map/all_to_all | solution.py:235
  52.1 0.6 %fusion = (bf16[32,256]{1,0:T(8,128)(2,1)}, bf16[32,256]{1,0:T(8,128)(2,1)}) fusion(bf16[32,512]{1,0:T(8,128)(2,1)S(1)} %reduce_sum.12), kind=kLoop, calls=%fused_computation.1 | loop fusion | bytes 65536 | tf_op jit(solution)/shard_map/slice | solution.py:237
  (1 shorter events, 0.0 us)
Async XLA Ops:
  0.6 16.5 %copy-start = (s32[1,128]{1,0:T(1,128)S(1)}, s32[1,128]{1,0:T(1,128)}, u32[]{:S(2)}) copy-start(s32[1,128]{1,0:T(1,128)} %ids.3) | copy-start | bytes 1540
  1.5 15.6 %collective-permute-start = (bf16[128,512]{1,0:T(8,128)(2,1)S(1)}, bf16[128,512]{1,0:T(8,128)(2,1)S(1)}, u32[]{:S(2)}, u32[]{:S(2)}) collective-permute-start(bf16[128,512]{1,0:T(8,128)(2,1)S(1)} %join.1.refs_0_), channel_id=1, source_target_pairs={{0,12},{4,16},{8,20},{12,24},{16,28},{20,32},{24,36},{28,40},{32,4... | collective-permute-start | bytes 393224 | tf_op jit(solution)/shard_map/ppermute | solution.py:219
  5.3 18.9 %collective-permute-start.2 = (bf16[128,512]{1,0:T(8,128)(2,1)S(1)}, bf16[128,512]{1,0:T(8,128)(2,1)S(1)}, u32[]{:S(2)}, u32[]{:S(2)}) collective-permute-start(bf16[128,512]{1,0:T(8,128)(2,1)S(1)} %join.1.refs_0_), channel_id=1, source_target_pairs={{0,4},{4,8},{8,12},{12,16},{16,20},{20,24},{24,28},{28,32},{32,36}... | collective-permute-start | bytes 393224 | tf_op jit(solution)/shard_map/ppermute | solution.py:219
  9.7 14.5 %collective-permute-start.1 = (bf16[128,512]{1,0:T(8,128)(2,1)S(1)}, bf16[128,512]{1,0:T(8,128)(2,1)S(1)}, u32[]{:S(2)}, u32[]{:S(2)}) collective-permute-start(bf16[128,512]{1,0:T(8,128)(2,1)S(1)} %join.1.refs_0_), channel_id=1, source_target_pairs={{0,8},{4,12},{8,16},{12,20},{16,24},{20,28},{24,32},{28,36},{32,40... | collective-permute-start | bytes 393224 | tf_op jit(solution)/shard_map/ppermute | solution.py:219
  19.0 17.6 %collective-permute-start.5 = (bf16[128,512]{1,0:T(8,128)(2,1)S(1)}, bf16[128,512]{1,0:T(8,128)(2,1)S(1)}, u32[]{:S(2)}, u32[]{:S(2)}) collective-permute-start(bf16[128,512]{1,0:T(8,128)(2,1)S(1)} %get-tuple-element.24), channel_id=1, source_target_pairs={{12,0},{16,4},{20,8},{24,12},{28,16},{32,20},{36,24},{40,28},{44,3... | collective-permute-start | bytes 393224 | tf_op jit(solution)/shard_map/ppermute | solution.py:219
  27.1 9.5 %collective-permute-start.3 = (bf16[128,512]{1,0:T(8,128)(2,1)S(1)}, bf16[128,512]{1,0:T(8,128)(2,1)S(1)}, u32[]{:S(2)}, u32[]{:S(2)}) collective-permute-start(bf16[128,512]{1,0:T(8,128)(2,1)S(1)} %get-tuple-element.22), channel_id=1, source_target_pairs={{4,0},{8,4},{12,8},{16,12},{20,16},{24,20},{28,24},{32,28},{36,32}... | collective-permute-start | bytes 393224 | tf_op jit(solution)/shard_map/ppermute | solution.py:219
  29.6 7.6 %collective-permute-start.4 = (bf16[128,512]{1,0:T(8,128)(2,1)S(1)}, bf16[128,512]{1,0:T(8,128)(2,1)S(1)}, u32[]{:S(2)}, u32[]{:S(2)}) collective-permute-start(bf16[128,512]{1,0:T(8,128)(2,1)S(1)} %get-tuple-element.23), channel_id=1, source_target_pairs={{8,0},{12,4},{16,8},{20,12},{24,16},{28,20},{32,24},{36,28},{40,32... | collective-permute-start | bytes 393224 | tf_op jit(solution)/shard_map/ppermute | solution.py:219

commit v4 on v3

--- a/solution.py
+++ b/solution.py
@@ -126,14 +126,10 @@
         part[:, (g + 2) * HD : (g + 3) * HD] = value_grad[rows].astype(part.dtype)
 
 
-def distances(ids, blocks):
+def in_document(ids, back):
     me = lax.axis_index("ctx")
-    away = []
-    for back in blocks:
-        at = jnp.maximum(me - back, 0)
-        live = jnp.logical_and(me >= back, ids[0, at] == ids[0, me])
-        away.append(jnp.where(live, F32(0.0), F32(FAR)))
-    return away
+    at = jnp.maximum(me - back, 0)
+    return jnp.logical_and(me >= back, ids[0, at] == ids[0, me])
 
 
 def load_kernel(*refs):
@@ -160,9 +156,19 @@
 def behind_kernel(blocks, ids, q, o, sums, delta, *refs):
     n = len(blocks)
     both, dscores, parts, probs = refs[:n], refs[n], refs[n + 1 : -1], refs[-1]
-    away = distances(ids, blocks)
-    for g in range(2):
-        grad_tiles(g, both, away, None, q, o, sums, delta, dscores, parts, probs)
+    live = [in_document(ids, back) for back in blocks]
+    away = [jnp.where(a, F32(0.0), F32(FAR)) for a in live]
+    nearest = live[blocks.index(min(blocks))]
+
+    @pl.when(nearest)
+    def _():
+        for g in range(2):
+            grad_tiles(g, both, away, None, q, o, sums, delta, dscores, parts, probs)
+
+    @pl.when(jnp.logical_not(nearest))
+    def _():
+        for ref in (dscores, *parts):
+            ref[...] = jnp.zeros_like(ref)
 
 
 def behind(name, blocks, ids, q, o, sums, delta, both):

time: 53 us -> 52.2 us (0.985)
  Pallas kernels: 10.2 us -> 9.01 us
    pallas_call x2, Pallas kernels: 4.75 us -> 3.57 us  [behind(): pl.pallas_call(functools.partial(behind_kernel, blocks), out_shape=[SHAPE...]
  transfers between devices with their start and end apart: 6 -> 6, of which waited for: 2 -> 2; matrix products, arithmetic and copies ran while one was open for 0% -> 0% of each run, Pallas kernels for 18% -> 16%
where the time goes in v4:
time: 52.2 us; the launch traced here: 51.5 us
  starting transfers between devices  24.1 us (46%)
  blocking collectives  15.1 us (29%)
  Pallas kernels  9.01 us (17%)
  waiting for transfers between devices  1.83 us (4%)
  between operations  0.77 us (1%)
  local copies, waits for them, and re-layouts  0.62 us (1%)
    ppermute x6, starting transfers between devices, shifted(): lax.ppermute(block, 'ctx', [(i, i + by) for i in devices if i + by in dev...  24.1 us
    all_to_all x1, blocking collectives, per_device(): arrived = lax.all_to_all(pieces, 'rec', 0, 0, tiled=True)  15.1 us
    pallas_call x2, Pallas kernels, behind(): pl.pallas_call(functools.partial(behind_kernel, blocks), out_shape=[SHAPE...  3.57 us
    pallas_call x1, Pallas kernels, own(): pl.pallas_call(own_kernel, out_shape=[SHAPE(q.shape, BF16), SHAPE((TOK, 4...  2.95 us
    ppermute x6, waiting for transfers between devices, shifted(): lax.ppermute(block, 'ctx', [(i, i + by) for i in devices if i + by in dev...  1.83 us
    pallas_call x1, Pallas kernels, load(): pl.pallas_call(load_kernel, out_shape=[SHAPE(a.shape, a.dtype) for a in a...  1.58 us
  transfers between devices with their start and end apart: 6, of which 2 were waited for; matrix products, arithmetic and copies ran while one was open for 0% of the time, Pallas kernels for 16%

profile of v4, /device:TPU:6, one launch (start us, length us, event | category | flops | bytes accessed | tf_op | source)
XLA Modules:
  0.0 51.5 jit_solution(12512824889224538533)
XLA Ops:
  0.6 0.0 copy-start
  0.6 0.9 %join.1.refs_0_ = bf16[128,512]{1,0:T(8,128)(2,1)S(1)} custom-call(bf16[128,256]{1,0:T(8,128)(2,1)} %k.1, bf16[128,256]{1,0:T(8,128)(2,1)} %v.1), custom_call_target="tpu_custom_call" | custom-call | bytes 2097152 | tf_op jit(solution)/shard_map/join/pallas_call | solution.py:73
  1.5 3.7 %collective-permute-start = (bf16[128,512]{1,0:T(8,128)(2,1)S(1)}, bf16[128,512]{1,0:T(8,128)(2,1)S(1)}, u32[]{:S(2)}, u32[]{:S(2)}) collective-permute-start(bf16[128,512]{1,0:T(8,128)(2,1)S(1)} %join.1.refs_0_), channel_id=1, source_target_pairs={{0,12},{4,16},{8,20},{12,24},{16,28},{20,32},{24,36},{28,40},{32,4... | collective-permute-start | bytes 393224 | tf_op jit(solution)/shard_map/ppermute | solution.py:225
  5.3 4.4 %collective-permute-start.2 = (bf16[128,512]{1,0:T(8,128)(2,1)S(1)}, bf16[128,512]{1,0:T(8,128)(2,1)S(1)}, u32[]{:S(2)}, u32[]{:S(2)}) collective-permute-start(bf16[128,512]{1,0:T(8,128)(2,1)S(1)} %join.1.refs_0_), channel_id=1, source_target_pairs={{0,4},{4,8},{8,12},{12,16},{16,20},{20,24},{24,28},{28,32},{32,36}... | collective-permute-start | bytes 393224 | tf_op jit(solution)/shard_map/ppermute | solution.py:225
  9.7 4.3 %collective-permute-start.1 = (bf16[128,512]{1,0:T(8,128)(2,1)S(1)}, bf16[128,512]{1,0:T(8,128)(2,1)S(1)}, u32[]{:S(2)}, u32[]{:S(2)}) collective-permute-start(bf16[128,512]{1,0:T(8,128)(2,1)S(1)} %join.1.refs_0_), channel_id=1, source_target_pairs={{0,8},{4,12},{8,16},{12,20},{16,24},{20,28},{24,32},{28,36},{32,40... | collective-permute-start | bytes 393224 | tf_op jit(solution)/shard_map/ppermute | solution.py:225
  14.0 1.6 %load.1 = (bf16[128,4096]{1,0:T(8,128)(2,1)S(1)}, bf16[128,4096]{1,0:T(8,128)(2,1)S(1)}, f32[32,128]{1,0:T(8,128)S(1)}, f32[32,128]{1,0:T(8,128)S(1)}) custom-call(bf16[128,4096]{1,0:T(8,128)(2,1)} %bitcast.6, bf16[128,4096]{1,0:T(8,128)(2,1)} %bitcast.7, f32[32,128]{1,0:T(8,128)} %bitcast.9, f32[32,128]{1,0:T(8,128)} %bitcast.10), custom_call_target="tpu_custom_call" | custom-call | flops 134217728 | bytes 2097152 | tf_op jit(solution)/shard_map/load/pallas_call | solution.py:146
  15.6 1.6 %collective-permute-done.refs_0_.refs_1_ = bf16[128,512]{1,0:T(8,128)(2,1)S(1)} collective-permute-done((bf16[128,512]{1,0:T(8,128)(2,1)S(1)}, bf16[128,512]{1,0:T(8,128)(2,1)S(1)}, u32[]{:S(2)}, u32[]{:S(2)}) %collective-permute-start) | collective-permute-done | bytes 131104 | tf_op jit(solution)/shard_map/ppermute | solution.py:225
  17.1 0.0 copy-done
  17.1 0.6 %early.1 = (bf16[128,4096]{1,0:T(8,128)(2,1)S(1)}, bf16[128,512]{1,0:T(8,128)(2,1)S(1)}) custom-call(s32[1,128]{1,0:T(1,128)S(1)} %copy-done, bf16[128,4096]{1,0:T(8,128)(2,1)S(1)} %get-tuple-element.14.q, bf16[128,4096]{1,0:T(8,128)(2,1)S(1)} %get-tuple-element.15.o, f32[32,128]{1,0:T(8,128)S(1)} %get-tuple-element.16.sums, ...), custom_call_target="tpu_custom_call" | custom-call | flops 536870912 | bytes 2097152 | tf_op jit(solution)/shard_map/early/pallas_call | solution.py:176
  17.8 5.2 %collective-permute-start.5 = (bf16[128,512]{1,0:T(8,128)(2,1)S(1)}, bf16[128,512]{1,0:T(8,128)(2,1)S(1)}, u32[]{:S(2)}, u32[]{:S(2)}) collective-permute-start(bf16[128,512]{1,0:T(8,128)(2,1)S(1)} %get-tuple-element.24), channel_id=1, source_target_pairs={{12,0},{16,4},{20,8},{24,12},{28,16},{32,20},{36,24},{40,28},{44,3... | collective-permute-start | bytes 393224 | tf_op jit(solution)/shard_map/ppermute | solution.py:225
  23.0 0.0 collective-permute-done.2.refs_1_.refs_3_
  23.0 0.0 collective-permute-done.1.refs_0_.refs_2_
  23.0 2.9 %late.1 = (bf16[256,4096]{1,0:T(8,128)(2,1)S(1)}, bf16[128,512]{1,0:T(8,128)(2,1)S(1)}, bf16[128,512]{1,0:T(8,128)(2,1)S(1)}) custom-call(s32[1,128]{1,0:T(1,128)S(1)} %copy-done, bf16[128,4096]{1,0:T(8,128)(2,1)S(1)} %get-tuple-element.14.q, bf16[128,4096]{1,0:T(8,128)(2,1)S(1)} %get-tuple-element.15.o, f32[32,128]{1,0:T(8,128)S(1)} %get-tuple-element.16.sums, ...), custom_call_target="tpu_custom_call" | custom-call | flops 1073741824 | bytes 2097152 | tf_op jit(solution)/shard_map/late/pallas_call | solution.py:176
  26.0 1.9 %collective-permute-start.3 = (bf16[128,512]{1,0:T(8,128)(2,1)S(1)}, bf16[128,512]{1,0:T(8,128)(2,1)S(1)}, u32[]{:S(2)}, u32[]{:S(2)}) collective-permute-start(bf16[128,512]{1,0:T(8,128)(2,1)S(1)} %get-tuple-element.22), channel_id=1, source_target_pairs={{4,0},{8,4},{12,8},{16,12},{20,16},{24,20},{28,24},{32,28},{36,32}... | collective-permute-start | bytes 393224 | tf_op jit(solution)/shard_map/ppermute | solution.py:225
  27.9 4.6 %collective-permute-start.4 = (bf16[128,512]{1,0:T(8,128)(2,1)S(1)}, bf16[128,512]{1,0:T(8,128)(2,1)S(1)}, u32[]{:S(2)}, u32[]{:S(2)}) collective-permute-start(bf16[128,512]{1,0:T(8,128)(2,1)S(1)} %get-tuple-element.23), channel_id=1, source_target_pairs={{8,0},{12,4},{16,8},{20,12},{24,16},{28,20},{32,24},{36,28},{40,32... | collective-permute-start | bytes 393224 | tf_op jit(solution)/shard_map/ppermute | solution.py:225
  32.5 3.0 %own.1 = (bf16[128,4096]{1,0:T(8,128)(2,1)}, f32[128,512]{1,0:T(8,128)S(1)}) custom-call(bf16[128,4096]{1,0:T(8,128)(2,1)S(1)} %get-tuple-element.14.q, bf16[128,4096]{1,0:T(8,128)(2,1)S(1)} %get-tuple-element.15.o, f32[32,128]{1,0:T(8,128)S(1)} %get-tuple-element.16.sums, f32[32,128]{1,0:T(8,128)S(1)} %get-tuple-element.17.delta, ...), custom_call_target="tpu_custom_call" | custom-call | flops 1073741824 | bytes 2097152 | tf_op jit(solution)/shard_map/own/pallas_call | solution.py:208
  35.4 0.0 collective-permute-done.5
  35.4 0.0 collective-permute-done.3
  35.4 0.2 collective-permute-done.4
  35.7 0.1 add_convert_fusion
  35.7 15.1 %all_to_all.5 = bf16[4,32,512]{2,1,0:T(8,128)(2,1)S(1)} all-to-all(bf16[4,32,512]{2,1,0:T(8,128)(2,1)S(1)} %bitcast.8), channel_id=1, replica_groups=mesh['ctx'=128,'rec'=4] {'rec'}, dimensions={0} | all-to-all | bytes 262144 | tf_op jit(solution)/shard_map/all_to_all | solution.py:241
  50.9 0.6 %fusion = (bf16[32,256]{1,0:T(8,128)(2,1)}, bf16[32,256]{1,0:T(8,128)(2,1)}) fusion(bf16[32,512]{1,0:T(8,128)(2,1)S(1)} %reduce_sum.12), kind=kLoop, calls=%fused_computation.1 | loop fusion | bytes 65536 | tf_op jit(solution)/shard_map/slice | solution.py:243
  (1 shorter events, 0.0 us)
Async XLA Ops:
  0.6 16.5 %copy-start = (s32[1,128]{1,0:T(1,128)S(1)}, s32[1,128]{1,0:T(1,128)}, u32[]{:S(2)}) copy-start(s32[1,128]{1,0:T(1,128)} %ids.3) | copy-start | bytes 1540
  1.5 15.6 %collective-permute-start = (bf16[128,512]{1,0:T(8,128)(2,1)S(1)}, bf16[128,512]{1,0:T(8,128)(2,1)S(1)}, u32[]{:S(2)}, u32[]{:S(2)}) collective-permute-start(bf16[128,512]{1,0:T(8,128)(2,1)S(1)} %join.1.refs_0_), channel_id=1, source_target_pairs={{0,12},{4,16},{8,20},{12,24},{16,28},{20,32},{24,36},{28,40},{32,4... | collective-permute-start | bytes 393224 | tf_op jit(solution)/shard_map/ppermute | solution.py:225
  5.3 17.7 %collective-permute-start.2 = (bf16[128,512]{1,0:T(8,128)(2,1)S(1)}, bf16[128,512]{1,0:T(8,128)(2,1)S(1)}, u32[]{:S(2)}, u32[]{:S(2)}) collective-permute-start(bf16[128,512]{1,0:T(8,128)(2,1)S(1)} %join.1.refs_0_), channel_id=1, source_target_pairs={{0,4},{4,8},{8,12},{12,16},{16,20},{20,24},{24,28},{28,32},{32,36}... | collective-permute-start | bytes 393224 | tf_op jit(solution)/shard_map/ppermute | solution.py:225
  9.7 13.3 %collective-permute-start.1 = (bf16[128,512]{1,0:T(8,128)(2,1)S(1)}, bf16[128,512]{1,0:T(8,128)(2,1)S(1)}, u32[]{:S(2)}, u32[]{:S(2)}) collective-permute-start(bf16[128,512]{1,0:T(8,128)(2,1)S(1)} %join.1.refs_0_), channel_id=1, source_target_pairs={{0,8},{4,12},{8,16},{12,20},{16,24},{20,28},{24,32},{28,36},{32,40... | collective-permute-start | bytes 393224 | tf_op jit(solution)/shard_map/ppermute | solution.py:225
  17.8 17.6 %collective-permute-start.5 = (bf16[128,512]{1,0:T(8,128)(2,1)S(1)}, bf16[128,512]{1,0:T(8,128)(2,1)S(1)}, u32[]{:S(2)}, u32[]{:S(2)}) collective-permute-start(bf16[128,512]{1,0:T(8,128)(2,1)S(1)} %get-tuple-element.24), channel_id=1, source_target_pairs={{12,0},{16,4},{20,8},{24,12},{28,16},{32,20},{36,24},{40,28},{44,3... | collective-permute-start | bytes 393224 | tf_op jit(solution)/shard_map/ppermute | solution.py:225
  26.0 9.5 %collective-permute-start.3 = (bf16[128,512]{1,0:T(8,128)(2,1)S(1)}, bf16[128,512]{1,0:T(8,128)(2,1)S(1)}, u32[]{:S(2)}, u32[]{:S(2)}) collective-permute-start(bf16[128,512]{1,0:T(8,128)(2,1)S(1)} %get-tuple-element.22), channel_id=1, source_target_pairs={{4,0},{8,4},{12,8},{16,12},{20,16},{24,20},{28,24},{32,28},{36,32}... | collective-permute-start | bytes 393224 | tf_op jit(solution)/shard_map/ppermute | solution.py:225
  27.9 7.8 %collective-permute-start.4 = (bf16[128,512]{1,0:T(8,128)(2,1)S(1)}, bf16[128,512]{1,0:T(8,128)(2,1)S(1)}, u32[]{:S(2)}, u32[]{:S(2)}) collective-permute-start(bf16[128,512]{1,0:T(8,128)(2,1)S(1)} %get-tuple-element.23), channel_id=1, source_target_pairs={{8,0},{12,4},{16,8},{20,12},{24,16},{28,20},{32,24},{36,28},{40,32... | collective-permute-start | bytes 393224 | tf_op jit(solution)/shard_map/ppermute | solution.py:225

commit v5 on v4

--- a/solution.py
+++ b/solution.py
@@ -158,17 +158,23 @@
     both, dscores, parts, probs = refs[:n], refs[n], refs[n + 1 : -1], refs[-1]
     live = [in_document(ids, back) for back in blocks]
     away = [jnp.where(a, F32(0.0), F32(FAR)) for a in live]
-    nearest = live[blocks.index(min(blocks))]
-
-    @pl.when(nearest)
-    def _():
-        for g in range(2):
-            grad_tiles(g, both, away, None, q, o, sums, delta, dscores, parts, probs)
-
-    @pl.when(jnp.logical_not(nearest))
-    def _():
-        for ref in (dscores, *parts):
-            ref[...] = jnp.zeros_like(ref)
+    for dead in range(n + 1):
+        rows = pl.ds(dead * TOK, (n - dead) * TOK)
+        here = True if dead == n else live[dead]
+        if dead:
+            here = jnp.logical_and(here, jnp.logical_not(live[dead - 1]))
+
+        @pl.when(here)
+        def _():
+            if dead:
+                dscores[: dead * TOK] = jnp.zeros((dead * TOK, WIDTH), BF16)
+            for part in parts[:dead]:
+                part[...] = jnp.zeros_like(part)
+            for g in range(2 if dead < n else 0):
+                grad_tiles(
+                    g, both[dead:], away[dead:], None, q, o, sums, delta,
+                    dscores.at[rows], parts[dead:], probs.at[rows],
+                )
 
 
 def behind(name, blocks, ids, q, o, sums, delta, both):

time: 52.2 us -> 52 us (level)
  the two profiles are of different devices: /device:TPU:6 before, /device:TPU:4 now
where the time goes in v5:
time: 52 us; the launch traced here: 51.6 us
  starting transfers between devices  24.3 us (47%)
  blocking collectives  15.8 us (30%)
  Pallas kernels  6.79 us (13%)
  waiting for transfers between devices  3.25 us (6%)
  between operations  0.76 us (1%)
  local copies, waits for them, and re-layouts  0.62 us (1%)
    ppermute x6, starting transfers between devices, shifted(): lax.ppermute(block, 'ctx', [(i, i + by) for i in devices if i + by in dev...  24.3 us
    all_to_all x1, blocking collectives, per_device(): arrived = lax.all_to_all(pieces, 'rec', 0, 0, tiled=True)  15.8 us
    ppermute x6, waiting for transfers between devices, shifted(): lax.ppermute(block, 'ctx', [(i, i + by) for i in devices if i + by in dev...  3.25 us
    pallas_call x1, Pallas kernels, own(): pl.pallas_call(own_kernel, out_shape=[SHAPE(q.shape, BF16), SHAPE((TOK, 4...  2.95 us
    pallas_call x1, Pallas kernels, load(): pl.pallas_call(load_kernel, out_shape=[SHAPE(a.shape, a.dtype) for a in a...  1.58 us
    pallas_call x2, Pallas kernels, behind(): pl.pallas_call(functools.partial(behind_kernel, blocks), out_shape=[SHAPE...  1.36 us
  transfers between devices with their start and end apart: 6, of which 2 were waited for; matrix products, arithmetic and copies ran while one was open for 0% of the time, Pallas kernels for 11%

profile of v5, /device:TPU:4, one launch (start us, length us, event | category | flops | bytes accessed | tf_op | source)
XLA Modules:
  0.0 51.6 jit_solution(4040892530263497658)
XLA Ops:
  0.6 0.0 copy-start
  0.6 0.9 %join.1.refs_0_ = bf16[128,512]{1,0:T(8,128)(2,1)S(1)} custom-call(bf16[128,256]{1,0:T(8,128)(2,1)} %k.1, bf16[128,256]{1,0:T(8,128)(2,1)} %v.1), custom_call_target="tpu_custom_call" | custom-call | bytes 2097152 | tf_op jit(solution)/shard_map/join/pallas_call | solution.py:73
  1.5 3.7 %collective-permute-start = (bf16[128,512]{1,0:T(8,128)(2,1)S(1)}, bf16[128,512]{1,0:T(8,128)(2,1)S(1)}, u32[]{:S(2)}, u32[]{:S(2)}) collective-permute-start(bf16[128,512]{1,0:T(8,128)(2,1)S(1)} %join.1.refs_0_), channel_id=1, source_target_pairs={{0,12},{4,16},{8,20},{12,24},{16,28},{20,32},{24,36},{28,40},{32,4... | collective-permute-start | bytes 393224 | tf_op jit(solution)/shard_map/ppermute | solution.py:231
  5.3 4.4 %collective-permute-start.2 = (bf16[128,512]{1,0:T(8,128)(2,1)S(1)}, bf16[128,512]{1,0:T(8,128)(2,1)S(1)}, u32[]{:S(2)}, u32[]{:S(2)}) collective-permute-start(bf16[128,512]{1,0:T(8,128)(2,1)S(1)} %join.1.refs_0_), channel_id=1, source_target_pairs={{0,4},{4,8},{8,12},{12,16},{16,20},{20,24},{24,28},{28,32},{32,36}... | collective-permute-start | bytes 393224 | tf_op jit(solution)/shard_map/ppermute | solution.py:231
  9.7 4.3 %collective-permute-start.1 = (bf16[128,512]{1,0:T(8,128)(2,1)S(1)}, bf16[128,512]{1,0:T(8,128)(2,1)S(1)}, u32[]{:S(2)}, u32[]{:S(2)}) collective-permute-start(bf16[128,512]{1,0:T(8,128)(2,1)S(1)} %join.1.refs_0_), channel_id=1, source_target_pairs={{0,8},{4,12},{8,16},{12,20},{16,24},{20,28},{24,32},{28,36},{32,40... | collective-permute-start | bytes 393224 | tf_op jit(solution)/shard_map/ppermute | solution.py:231
  14.0 1.6 %load.1 = (bf16[128,4096]{1,0:T(8,128)(2,1)S(1)}, bf16[128,4096]{1,0:T(8,128)(2,1)S(1)}, f32[32,128]{1,0:T(8,128)S(1)}, f32[32,128]{1,0:T(8,128)S(1)}) custom-call(bf16[128,4096]{1,0:T(8,128)(2,1)} %bitcast.6, bf16[128,4096]{1,0:T(8,128)(2,1)} %bitcast.7, f32[32,128]{1,0:T(8,128)} %bitcast.9, f32[32,128]{1,0:T(8,128)} %bitcast.10), custom_call_target="tpu_custom_call" | custom-call | flops 134217728 | bytes 2097152 | tf_op jit(solution)/shard_map/load/pallas_call | solution.py:146
  15.6 1.3 %collective-permute-done.refs_0_.refs_1_ = bf16[128,512]{1,0:T(8,128)(2,1)S(1)} collective-permute-done((bf16[128,512]{1,0:T(8,128)(2,1)S(1)}, bf16[128,512]{1,0:T(8,128)(2,1)S(1)}, u32[]{:S(2)}, u32[]{:S(2)}) %collective-permute-start) | collective-permute-done | bytes 131104 | tf_op jit(solution)/shard_map/ppermute | solution.py:231
  16.8 0.0 copy-done
  16.9 0.6 %early.1 = (bf16[128,4096]{1,0:T(8,128)(2,1)S(1)}, bf16[128,512]{1,0:T(8,128)(2,1)S(1)}) custom-call(s32[1,128]{1,0:T(1,128)S(1)} %copy-done, bf16[128,4096]{1,0:T(8,128)(2,1)S(1)} %get-tuple-element.14.q, bf16[128,4096]{1,0:T(8,128)(2,1)S(1)} %get-tuple-element.15.o, f32[32,128]{1,0:T(8,128)S(1)} %get-tuple-element.16.sums, ...), custom_call_target="tpu_custom_call" | custom-call | flops 536870912 | bytes 2097152 | tf_op jit(solution)/shard_map/early/pallas_call | solution.py:182
  17.5 5.2 %collective-permute-start.5 = (bf16[128,512]{1,0:T(8,128)(2,1)S(1)}, bf16[128,512]{1,0:T(8,128)(2,1)S(1)}, u32[]{:S(2)}, u32[]{:S(2)}) collective-permute-start(bf16[128,512]{1,0:T(8,128)(2,1)S(1)} %get-tuple-element.24), channel_id=1, source_target_pairs={{12,0},{16,4},{20,8},{24,12},{28,16},{32,20},{36,24},{40,28},{44,3... | collective-permute-start | bytes 393224 | tf_op jit(solution)/shard_map/ppermute | solution.py:231
  22.7 0.0 collective-permute-done.2.refs_1_.refs_3_
  22.7 0.0 collective-permute-done.1.refs_0_.refs_2_
  22.7 0.7 %late.1 = (bf16[256,4096]{1,0:T(8,128)(2,1)S(1)}, bf16[128,512]{1,0:T(8,128)(2,1)S(1)}, bf16[128,512]{1,0:T(8,128)(2,1)S(1)}) custom-call(s32[1,128]{1,0:T(1,128)S(1)} %copy-done, bf16[128,4096]{1,0:T(8,128)(2,1)S(1)} %get-tuple-element.14.q, bf16[128,4096]{1,0:T(8,128)(2,1)S(1)} %get-tuple-element.15.o, f32[32,128]{1,0:T(8,128)S(1)} %get-tuple-element.16.sums, ...), custom_call_target="tpu_custom_call" | custom-call | flops 1073741824 | bytes 2097152 | tf_op jit(solution)/shard_map/late/pallas_call | solution.py:182
  23.4 4.8 %collective-permute-start.3 = (bf16[128,512]{1,0:T(8,128)(2,1)S(1)}, bf16[128,512]{1,0:T(8,128)(2,1)S(1)}, u32[]{:S(2)}, u32[]{:S(2)}) collective-permute-start(bf16[128,512]{1,0:T(8,128)(2,1)S(1)} %get-tuple-element.22), channel_id=1, source_target_pairs={{4,0},{8,4},{12,8},{16,12},{20,16},{24,20},{28,24},{32,28},{36,32}... | collective-permute-start | bytes 393224 | tf_op jit(solution)/shard_map/ppermute | solution.py:231
  28.3 1.9 %collective-permute-start.4 = (bf16[128,512]{1,0:T(8,128)(2,1)S(1)}, bf16[128,512]{1,0:T(8,128)(2,1)S(1)}, u32[]{:S(2)}, u32[]{:S(2)}) collective-permute-start(bf16[128,512]{1,0:T(8,128)(2,1)S(1)} %get-tuple-element.23), channel_id=1, source_target_pairs={{8,0},{12,4},{16,8},{20,12},{24,16},{28,20},{32,24},{36,28},{40,32... | collective-permute-start | bytes 393224 | tf_op jit(solution)/shard_map/ppermute | solution.py:231
  30.2 3.0 %own.1 = (bf16[128,4096]{1,0:T(8,128)(2,1)}, f32[128,512]{1,0:T(8,128)S(1)}) custom-call(bf16[128,4096]{1,0:T(8,128)(2,1)S(1)} %get-tuple-element.14.q, bf16[128,4096]{1,0:T(8,128)(2,1)S(1)} %get-tuple-element.15.o, f32[32,128]{1,0:T(8,128)S(1)} %get-tuple-element.16.sums, f32[32,128]{1,0:T(8,128)S(1)} %get-tuple-element.17.delta, ...), custom_call_target="tpu_custom_call" | custom-call | flops 1073741824 | bytes 2097152 | tf_op jit(solution)/shard_map/own/pallas_call | solution.py:214
  33.2 0.0 collective-permute-done.5
  33.2 0.0 collective-permute-done.3
  33.2 1.9 %collective-permute-done.4 = bf16[128,512]{1,0:T(8,128)(2,1)S(1)} collective-permute-done((bf16[128,512]{1,0:T(8,128)(2,1)S(1)}, bf16[128,512]{1,0:T(8,128)(2,1)S(1)}, u32[]{:S(2)}, u32[]{:S(2)}) %collective-permute-start.4) | collective-permute-done | bytes 131104 | tf_op jit(solution)/shard_map/ppermute | solution.py:231
  35.1 0.1 add_convert_fusion
  35.2 15.8 %all_to_all.5 = bf16[4,32,512]{2,1,0:T(8,128)(2,1)S(1)} all-to-all(bf16[4,32,512]{2,1,0:T(8,128)(2,1)S(1)} %bitcast.8), channel_id=1, replica_groups=mesh['ctx'=128,'rec'=4] {'rec'}, dimensions={0} | all-to-all | bytes 262144 | tf_op jit(solution)/shard_map/all_to_all | solution.py:247
  51.0 0.6 %fusion = (bf16[32,256]{1,0:T(8,128)(2,1)}, bf16[32,256]{1,0:T(8,128)(2,1)}) fusion(bf16[32,512]{1,0:T(8,128)(2,1)S(1)} %reduce_sum.12), kind=kLoop, calls=%fused_computation.1 | loop fusion | bytes 65536 | tf_op jit(solution)/shard_map/slice | solution.py:249
  (1 shorter events, 0.0 us)
Async XLA Ops:
  0.6 16.2 %copy-start = (s32[1,128]{1,0:T(1,128)S(1)}, s32[1,128]{1,0:T(1,128)}, u32[]{:S(2)}) copy-start(s32[1,128]{1,0:T(1,128)} %ids.3) | copy-start | bytes 1540
  1.5 15.3 %collective-permute-start = (bf16[128,512]{1,0:T(8,128)(2,1)S(1)}, bf16[128,512]{1,0:T(8,128)(2,1)S(1)}, u32[]{:S(2)}, u32[]{:S(2)}) collective-permute-start(bf16[128,512]{1,0:T(8,128)(2,1)S(1)} %join.1.refs_0_), channel_id=1, source_target_pairs={{0,12},{4,16},{8,20},{12,24},{16,28},{20,32},{24,36},{28,40},{32,4... | collective-permute-start | bytes 393224 | tf_op jit(solution)/shard_map/ppermute | solution.py:231
  5.3 17.4 %collective-permute-start.2 = (bf16[128,512]{1,0:T(8,128)(2,1)S(1)}, bf16[128,512]{1,0:T(8,128)(2,1)S(1)}, u32[]{:S(2)}, u32[]{:S(2)}) collective-permute-start(bf16[128,512]{1,0:T(8,128)(2,1)S(1)} %join.1.refs_0_), channel_id=1, source_target_pairs={{0,4},{4,8},{8,12},{12,16},{16,20},{20,24},{24,28},{28,32},{32,36}... | collective-permute-start | bytes 393224 | tf_op jit(solution)/shard_map/ppermute | solution.py:231
  9.7 13.0 %collective-permute-start.1 = (bf16[128,512]{1,0:T(8,128)(2,1)S(1)}, bf16[128,512]{1,0:T(8,128)(2,1)S(1)}, u32[]{:S(2)}, u32[]{:S(2)}) collective-permute-start(bf16[128,512]{1,0:T(8,128)(2,1)S(1)} %join.1.refs_0_), channel_id=1, source_target_pairs={{0,8},{4,12},{8,16},{12,20},{16,24},{20,28},{24,32},{28,36},{32,40... | collective-permute-start | bytes 393224 | tf_op jit(solution)/shard_map/ppermute | solution.py:231
  17.5 15.7 %collective-permute-start.5 = (bf16[128,512]{1,0:T(8,128)(2,1)S(1)}, bf16[128,512]{1,0:T(8,128)(2,1)S(1)}, u32[]{:S(2)}, u32[]{:S(2)}) collective-permute-start(bf16[128,512]{1,0:T(8,128)(2,1)S(1)} %get-tuple-element.24), channel_id=1, source_target_pairs={{12,0},{16,4},{20,8},{24,12},{28,16},{32,20},{36,24},{40,28},{44,3... | collective-permute-start | bytes 393224 | tf_op jit(solution)/shard_map/ppermute | solution.py:231
  23.4 9.7 %collective-permute-start.3 = (bf16[128,512]{1,0:T(8,128)(2,1)S(1)}, bf16[128,512]{1,0:T(8,128)(2,1)S(1)}, u32[]{:S(2)}, u32[]{:S(2)}) collective-permute-start(bf16[128,512]{1,0:T(8,128)(2,1)S(1)} %get-tuple-element.22), channel_id=1, source_target_pairs={{4,0},{8,4},{12,8},{16,12},{20,16},{24,20},{28,24},{32,28},{36,32}... | collective-permute-start | bytes 393224 | tf_op jit(solution)/shard_map/ppermute | solution.py:231
  28.3 6.9 %collective-permute-start.4 = (bf16[128,512]{1,0:T(8,128)(2,1)S(1)}, bf16[128,512]{1,0:T(8,128)(2,1)S(1)}, u32[]{:S(2)}, u32[]{:S(2)}) collective-permute-start(bf16[128,512]{1,0:T(8,128)(2,1)S(1)} %get-tuple-element.23), channel_id=1, source_target_pairs={{8,0},{12,4},{16,8},{20,12},{24,16},{28,20},{32,24},{36,28},{40,32... | collective-permute-start | bytes 393224 | tf_op jit(solution)/shard_map/ppermute | solution.py:231

commit v6 on v5

--- a/solution.py
+++ b/solution.py
@@ -13,7 +13,7 @@
 SPAN = 4
 HEADS = 32
 GROUP = 16
-CHUNK = 2
+CHUNK = 4
 WIDTH = HEADS * HD
 HALF = GROUP * HD
 SCALE = HD**-0.5

time: 52 us -> 51.7 us (level)
  the two profiles are of different devices: /device:TPU:4 before, /device:TPU:12 now
where the time goes in v6:
time: 51.7 us; the launch traced here: 51 us
  starting transfers between devices  24.1 us (47%)
  blocking collectives  16.6 us (32%)
  Pallas kernels  6.77 us (13%)
  waiting for transfers between devices  2.07 us (4%)
  between operations  0.76 us (1%)
  local copies, waits for them, and re-layouts  0.62 us (1%)
    ppermute x6, starting transfers between devices, shifted(): lax.ppermute(block, 'ctx', [(i, i + by) for i in devices if i + by in dev...  24.1 us
    all_to_all x1, blocking collectives, per_device(): arrived = lax.all_to_all(pieces, 'rec', 0, 0, tiled=True)  16.6 us
    pallas_call x1, Pallas kernels, own(): pl.pallas_call(own_kernel, out_shape=[SHAPE(q.shape, BF16), SHAPE((TOK, 4...  2.93 us
    ppermute x6, waiting for transfers between devices, shifted(): lax.ppermute(block, 'ctx', [(i, i + by) for i in devices if i + by in dev...  2.07 us
    pallas_call x1, Pallas kernels, load(): pl.pallas_call(load_kernel, out_shape=[SHAPE(a.shape, a.dtype) for a in a...  1.58 us
    pallas_call x2, Pallas kernels, behind(): pl.pallas_call(functools.partial(behind_kernel, blocks), out_shape=[SHAPE...  1.36 us
  transfers between devices with their start and end apart: 6, of which 2 were waited for; matrix products, arithmetic and copies ran while one was open for 0% of the time, Pallas kernels for 12%

profile of v6, /device:TPU:12, one launch (start us, length us, event | category | flops | bytes accessed | tf_op | source)
XLA Modules:
  0.0 51.0 jit_solution(18019316464022461848)
XLA Ops:
  0.6 0.0 copy-start
  0.6 0.9 %join.1.refs_0_ = bf16[128,512]{1,0:T(8,128)(2,1)S(1)} custom-call(bf16[128,256]{1,0:T(8,128)(2,1)} %k.1, bf16[128,256]{1,0:T(8,128)(2,1)} %v.1), custom_call_target="tpu_custom_call" | custom-call | bytes 2097152 | tf_op jit(solution)/shard_map/join/pallas_call | solution.py:73
  1.5 3.7 %collective-permute-start = (bf16[128,512]{1,0:T(8,128)(2,1)S(1)}, bf16[128,512]{1,0:T(8,128)(2,1)S(1)}, u32[]{:S(2)}, u32[]{:S(2)}) collective-permute-start(bf16[128,512]{1,0:T(8,128)(2,1)S(1)} %join.1.refs_0_), channel_id=1, source_target_pairs={{0,12},{4,16},{8,20},{12,24},{16,28},{20,32},{24,36},{28,40},{32,4... | collective-permute-start | bytes 393224 | tf_op jit(solution)/shard_map/ppermute | solution.py:231
  5.3 4.4 %collective-permute-start.2 = (bf16[128,512]{1,0:T(8,128)(2,1)S(1)}, bf16[128,512]{1,0:T(8,128)(2,1)S(1)}, u32[]{:S(2)}, u32[]{:S(2)}) collective-permute-start(bf16[128,512]{1,0:T(8,128)(2,1)S(1)} %join.1.refs_0_), channel_id=1, source_target_pairs={{0,4},{4,8},{8,12},{12,16},{16,20},{20,24},{24,28},{28,32},{32,36}... | collective-permute-start | bytes 393224 | tf_op jit(solution)/shard_map/ppermute | solution.py:231
  9.7 4.3 %collective-permute-start.1 = (bf16[128,512]{1,0:T(8,128)(2,1)S(1)}, bf16[128,512]{1,0:T(8,128)(2,1)S(1)}, u32[]{:S(2)}, u32[]{:S(2)}) collective-permute-start(bf16[128,512]{1,0:T(8,128)(2,1)S(1)} %join.1.refs_0_), channel_id=1, source_target_pairs={{0,8},{4,12},{8,16},{12,20},{16,24},{20,28},{24,32},{28,36},{32,40... | collective-permute-start | bytes 393224 | tf_op jit(solution)/shard_map/ppermute | solution.py:231
  14.0 1.6 %load.1 = (bf16[128,4096]{1,0:T(8,128)(2,1)S(1)}, bf16[128,4096]{1,0:T(8,128)(2,1)S(1)}, f32[32,128]{1,0:T(8,128)S(1)}, f32[32,128]{1,0:T(8,128)S(1)}) custom-call(bf16[128,4096]{1,0:T(8,128)(2,1)} %bitcast.6, bf16[128,4096]{1,0:T(8,128)(2,1)} %bitcast.7, f32[32,128]{1,0:T(8,128)} %bitcast.9, f32[32,128]{1,0:T(8,128)} %bitcast.10), custom_call_target="tpu_custom_call" | custom-call | flops 134217728 | bytes 2097152 | tf_op jit(solution)/shard_map/load/pallas_call | solution.py:146
  15.6 0.2 collective-permute-done.refs_0_.refs_1_
  15.8 0.0 copy-done
  15.8 0.6 %early.1 = (bf16[128,4096]{1,0:T(8,128)(2,1)S(1)}, bf16[128,512]{1,0:T(8,128)(2,1)S(1)}) custom-call(s32[1,128]{1,0:T(1,128)S(1)} %copy-done, bf16[128,4096]{1,0:T(8,128)(2,1)S(1)} %get-tuple-element.14.q, bf16[128,4096]{1,0:T(8,128)(2,1)S(1)} %get-tuple-element.15.o, f32[32,128]{1,0:T(8,128)S(1)} %get-tuple-element.16.sums, ...), custom_call_target="tpu_custom_call" | custom-call | flops 536870912 | bytes 2097152 | tf_op jit(solution)/shard_map/early/pallas_call | solution.py:182
  16.4 5.2 %collective-permute-start.5 = (bf16[128,512]{1,0:T(8,128)(2,1)S(1)}, bf16[128,512]{1,0:T(8,128)(2,1)S(1)}, u32[]{:S(2)}, u32[]{:S(2)}) collective-permute-start(bf16[128,512]{1,0:T(8,128)(2,1)S(1)} %get-tuple-element.24), channel_id=1, source_target_pairs={{12,0},{16,4},{20,8},{24,12},{28,16},{32,20},{36,24},{40,28},{44,3... | collective-permute-start | bytes 393224 | tf_op jit(solution)/shard_map/ppermute | solution.py:231
  21.6 0.0 collective-permute-done.2.refs_1_.refs_3_
  21.6 0.0 collective-permute-done.1.refs_0_.refs_2_
  21.6 0.7 %late.1 = (bf16[256,4096]{1,0:T(8,128)(2,1)S(1)}, bf16[128,512]{1,0:T(8,128)(2,1)S(1)}, bf16[128,512]{1,0:T(8,128)(2,1)S(1)}) custom-call(s32[1,128]{1,0:T(1,128)S(1)} %copy-done, bf16[128,4096]{1,0:T(8,128)(2,1)S(1)} %get-tuple-element.14.q, bf16[128,4096]{1,0:T(8,128)(2,1)S(1)} %get-tuple-element.15.o, f32[32,128]{1,0:T(8,128)S(1)} %get-tuple-element.16.sums, ...), custom_call_target="tpu_custom_call" | custom-call | flops 1073741824 | bytes 2097152 | tf_op jit(solution)/shard_map/late/pallas_call | solution.py:182
  22.4 4.0 %collective-permute-start.3 = (bf16[128,512]{1,0:T(8,128)(2,1)S(1)}, bf16[128,512]{1,0:T(8,128)(2,1)S(1)}, u32[]{:S(2)}, u32[]{:S(2)}) collective-permute-start(bf16[128,512]{1,0:T(8,128)(2,1)S(1)} %get-tuple-element.22), channel_id=1, source_target_pairs={{4,0},{8,4},{12,8},{16,12},{20,16},{24,20},{28,24},{32,28},{36,32}... | collective-permute-start | bytes 393224 | tf_op jit(solution)/shard_map/ppermute | solution.py:231
  26.4 2.4 %collective-permute-start.4 = (bf16[128,512]{1,0:T(8,128)(2,1)S(1)}, bf16[128,512]{1,0:T(8,128)(2,1)S(1)}, u32[]{:S(2)}, u32[]{:S(2)}) collective-permute-start(bf16[128,512]{1,0:T(8,128)(2,1)S(1)} %get-tuple-element.23), channel_id=1, source_target_pairs={{8,0},{12,4},{16,8},{20,12},{24,16},{28,20},{32,24},{36,28},{40,32... | collective-permute-start | bytes 393224 | tf_op jit(solution)/shard_map/ppermute | solution.py:231
  28.9 2.9 %own.1 = (bf16[128,4096]{1,0:T(8,128)(2,1)}, f32[128,512]{1,0:T(8,128)S(1)}) custom-call(bf16[128,4096]{1,0:T(8,128)(2,1)S(1)} %get-tuple-element.14.q, bf16[128,4096]{1,0:T(8,128)(2,1)S(1)} %get-tuple-element.15.o, f32[32,128]{1,0:T(8,128)S(1)} %get-tuple-element.16.sums, f32[32,128]{1,0:T(8,128)S(1)} %get-tuple-element.17.delta, ...), custom_call_target="tpu_custom_call" | custom-call | flops 1073741824 | bytes 2097152 | tf_op jit(solution)/shard_map/own/pallas_call | solution.py:214
  31.8 0.0 collective-permute-done.5
  31.8 0.0 collective-permute-done.3
  31.8 1.9 %collective-permute-done.4 = bf16[128,512]{1,0:T(8,128)(2,1)S(1)} collective-permute-done((bf16[128,512]{1,0:T(8,128)(2,1)S(1)}, bf16[128,512]{1,0:T(8,128)(2,1)S(1)}, u32[]{:S(2)}, u32[]{:S(2)}) %collective-permute-start.4) | collective-permute-done | bytes 131104 | tf_op jit(solution)/shard_map/ppermute | solution.py:231
  33.7 0.1 add_convert_fusion
  33.7 16.6 %all_to_all.5 = bf16[4,32,512]{2,1,0:T(8,128)(2,1)S(1)} all-to-all(bf16[4,32,512]{2,1,0:T(8,128)(2,1)S(1)} %bitcast.8), channel_id=1, replica_groups=mesh['ctx'=128,'rec'=4] {'rec'}, dimensions={0} | all-to-all | bytes 262144 | tf_op jit(solution)/shard_map/all_to_all | solution.py:247
  50.4 0.6 %fusion = (bf16[32,256]{1,0:T(8,128)(2,1)}, bf16[32,256]{1,0:T(8,128)(2,1)}) fusion(bf16[32,512]{1,0:T(8,128)(2,1)S(1)} %reduce_sum.12), kind=kLoop, calls=%fused_computation.1 | loop fusion | bytes 65536 | tf_op jit(solution)/shard_map/slice | solution.py:249
  (1 shorter events, 0.0 us)
Async XLA Ops:
  0.6 15.1 %copy-start = (s32[1,128]{1,0:T(1,128)S(1)}, s32[1,128]{1,0:T(1,128)}, u32[]{:S(2)}) copy-start(s32[1,128]{1,0:T(1,128)} %ids.3) | copy-start | bytes 1540
  1.5 14.2 %collective-permute-start = (bf16[128,512]{1,0:T(8,128)(2,1)S(1)}, bf16[128,512]{1,0:T(8,128)(2,1)S(1)}, u32[]{:S(2)}, u32[]{:S(2)}) collective-permute-start(bf16[128,512]{1,0:T(8,128)(2,1)S(1)} %join.1.refs_0_), channel_id=1, source_target_pairs={{0,12},{4,16},{8,20},{12,24},{16,28},{20,32},{24,36},{28,40},{32,4... | collective-permute-start | bytes 393224 | tf_op jit(solution)/shard_map/ppermute | solution.py:231
  5.3 16.3 %collective-permute-start.2 = (bf16[128,512]{1,0:T(8,128)(2,1)S(1)}, bf16[128,512]{1,0:T(8,128)(2,1)S(1)}, u32[]{:S(2)}, u32[]{:S(2)}) collective-permute-start(bf16[128,512]{1,0:T(8,128)(2,1)S(1)} %join.1.refs_0_), channel_id=1, source_target_pairs={{0,4},{4,8},{8,12},{12,16},{16,20},{20,24},{24,28},{28,32},{32,36}... | collective-permute-start | bytes 393224 | tf_op jit(solution)/shard_map/ppermute | solution.py:231
  9.7 11.9 %collective-permute-start.1 = (bf16[128,512]{1,0:T(8,128)(2,1)S(1)}, bf16[128,512]{1,0:T(8,128)(2,1)S(1)}, u32[]{:S(2)}, u32[]{:S(2)}) collective-permute-start(bf16[128,512]{1,0:T(8,128)(2,1)S(1)} %join.1.refs_0_), channel_id=1, source_target_pairs={{0,8},{4,12},{8,16},{12,20},{16,24},{20,28},{24,32},{28,36},{32,40... | collective-permute-start | bytes 393224 | tf_op jit(solution)/shard_map/ppermute | solution.py:231
  16.4 15.4 %collective-permute-start.5 = (bf16[128,512]{1,0:T(8,128)(2,1)S(1)}, bf16[128,512]{1,0:T(8,128)(2,1)S(1)}, u32[]{:S(2)}, u32[]{:S(2)}) collective-permute-start(bf16[128,512]{1,0:T(8,128)(2,1)S(1)} %get-tuple-element.24), channel_id=1, source_target_pairs={{12,0},{16,4},{20,8},{24,12},{28,16},{32,20},{36,24},{40,28},{44,3... | collective-permute-start | bytes 393224 | tf_op jit(solution)/shard_map/ppermute | solution.py:231
  22.4 9.5 %collective-permute-start.3 = (bf16[128,512]{1,0:T(8,128)(2,1)S(1)}, bf16[128,512]{1,0:T(8,128)(2,1)S(1)}, u32[]{:S(2)}, u32[]{:S(2)}) collective-permute-start(bf16[128,512]{1,0:T(8,128)(2,1)S(1)} %get-tuple-element.22), channel_id=1, source_target_pairs={{4,0},{8,4},{12,8},{16,12},{20,16},{24,20},{28,24},{32,28},{36,32}... | collective-permute-start | bytes 393224 | tf_op jit(solution)/shard_map/ppermute | solution.py:231
  26.4 7.3 %collective-permute-start.4 = (bf16[128,512]{1,0:T(8,128)(2,1)S(1)}, bf16[128,512]{1,0:T(8,128)(2,1)S(1)}, u32[]{:S(2)}, u32[]{:S(2)}) collective-permute-start(bf16[128,512]{1,0:T(8,128)(2,1)S(1)} %get-tuple-element.23), channel_id=1, source_target_pairs={{8,0},{12,4},{16,8},{20,12},{24,16},{28,20},{32,24},{36,28},{40,32... | collective-permute-start | bytes 393224 | tf_op jit(solution)/shard_map/ppermute | solution.py:231
